TPU v7x, 32 devices: a whole 2x2x4 slice. The times are simulated.
32 devices in a mesh: seq: 16 (over z, y, core), rows: 2 (over x).
Axes of the slice: x: 2, y: 2, z: 4, core: 2. Of those that a mesh axis runs over, the one named last changes fastest.
Arguments:
- tokens: bfloat16 [32, 16, 64, 1152], P('seq', 'rows'), may hold values from -6 to 6
- image_ids: int32 [32, 64], P('seq'), may hold values from 0 to 3, as said below
- timestep: int32 [32, 4], P('seq'), may hold values from 0 to 999
- norm1_gain: float32 [1152], replicated, may hold values from 0.1 to 1.9
- norm1_shift: float32 [1152], replicated, may hold values from -3 to 3
- time_in_weight: bfloat16 [256, 1152], P('seq'), may hold values from -0.375 to 0.375
- time_in_bias: float32 [1152], replicated, may hold values from -3 to 3
- time_out_weight: bfloat16 [1152, 1152], P('seq'), may hold values from -0.1875 to 0.1875
- time_out_bias: float32 [1152], replicated, may hold values from -3 to 3
- mix_weight: bfloat16 [1152, 3456], P('seq'), may hold values from -0.1875 to 0.1875
- time_mix_weight: bfloat16 [1152, 3456], P('seq'), may hold values from -0.1875 to 0.1875
- position_bias: float32 [16, 9, 9], replicated, may hold values from -4 to 4
- proj_weight: bfloat16 [1152, 1152], P('seq'), may hold values from -0.5 to 0.5
- proj_bias: float32 [1152], replicated, may hold values from -2 to 2
- norm2_gain: float32 [1152], replicated, may hold values from 0.1 to 1.9
- norm2_shift: float32 [1152], replicated, may hold values from -3 to 3
- up_weight: bfloat16 [1152, 4608], P('seq'), may hold values from -0.1875 to 0.1875
- up_bias: float32 [4608], replicated, may hold values from -3 to 3
- down_weight: bfloat16 [4608, 1152], P('seq'), may hold values from -0.09375 to 0.09375
- down_bias: float32 [1152], replicated, may hold values from -2 to 2
- cotangent: bfloat16 [32, 16, 64, 1152], P('seq', 'rows'), may hold values from -6 to 6
Outputs:
- output: bfloat16 [32, 16, 64, 1152], P('seq', 'rows')
- tokens_grad: bfloat16 [32, 16, 64, 1152], P('seq', 'rows')
- norm1_gain_grad: float32 [1152], replicated
- norm1_shift_grad: float32 [1152], replicated
- time_in_weight_grad: float32 [256, 1152], P('seq')
- time_in_bias_grad: float32 [1152], replicated
- time_out_weight_grad: float32 [1152, 1152], P('seq')
- time_out_bias_grad: float32 [1152], replicated
- mix_weight_grad: float32 [1152, 3456], P('seq')
- time_mix_weight_grad: float32 [1152, 3456], P('seq')
- position_bias_grad: float32 [16, 9, 9], replicated
- proj_weight_grad: float32 [1152, 1152], P('seq')
- proj_bias_grad: float32 [1152], replicated
- norm2_gain_grad: float32 [1152], replicated
- norm2_shift_grad: float32 [1152], replicated
- up_weight_grad: float32 [1152, 4608], P('seq')
- up_bias_grad: float32 [4608], replicated
- down_weight_grad: float32 [4608, 1152], P('seq')
- down_bias_grad: float32 [1152], replicated
Inputs may be any that keep to these rules, and one draw needn't show every extreme that they name: `image_ids`: canvas columns k * 16 to (k + 1) * 16 - 1 of a sequence row share one id, and the 4 blocks of a row hold each id once.
All inputs are finite; a program needn't handle non-finite values.
Results may differ from a plain program's by a relative error of at most 0.019.
Values may be sent and summed in bfloat16 or wider, within the bound.
No kernel may reach another device: no remote copies, remote signals or barrier semaphores. Data moves between devices by JAX's collectives and lax.ppermute only.
A program may use at most 640 MiB of HBM per device.

v0:
```python
import math

import jax
import jax.numpy as jnp
from jax import lax
from jax.sharding import PartitionSpec as P

D = 1152
HEADS = 16
HEAD_DIM = 72
FF = 4608
FREQ = 256
GRID = 16
PACK = 4
REACH = 4


epsilon = 1e-06
floor_score = -1e30
highest = lax.Precision.HIGHEST


def passed_along(block, axis, distance):
    devices = range(lax.axis_size(axis))
    route = [(i - distance, i) for i in devices if i - distance in devices]
    return lax.ppermute(block, axis, route)


def low_dot(left, right):
    return jnp.dot(left, right, preferred_element_type=jnp.float32)


def gelu_tanh(values):
    return jax.nn.gelu(values, approximate=True)


def norm_forward(values, norm_gain, norm_shift):
    centred = values - jnp.mean(values, axis=-1, keepdims=True)
    inverse = lax.rsqrt(jnp.mean(centred * centred, axis=-1, keepdims=True) + epsilon)
    unit_rows = centred * inverse
    return (unit_rows * norm_gain + norm_shift, unit_rows, inverse)


def norm_backward(grad_out, unit_rows, inverse, norm_gain):
    scaled = grad_out * norm_gain
    grad_in = inverse * (
        scaled
        - jnp.mean(scaled, axis=-1, keepdims=True)
        - unit_rows * jnp.mean(scaled * unit_rows, axis=-1, keepdims=True)
    )
    leading = tuple(range(grad_out.ndim - 1))
    return (grad_in, jnp.sum(grad_out * unit_rows, axis=leading), jnp.sum(grad_out, axis=leading))


def on_device(
    tokens,
    image_ids,
    timestep,
    norm1_gain,
    norm1_shift,
    time_in_weight,
    time_in_bias,
    time_out_weight,
    time_out_bias,
    mix_weight,
    time_mix_weight,
    position_bias,
    proj_weight,
    proj_bias,
    norm2_gain,
    norm2_shift,
    up_weight,
    up_bias,
    down_weight,
    down_bias,
    cotangent,
):
    seq_rows, local_rows, columns, _ = tokens.shape
    score_scale = HEAD_DIM ** (-0.5)
    full_tin, full_tout, full_mix, full_tmix, full_proj, full_up, full_down = (
        lax.all_gather(time_in_weight, "seq", axis=0, tiled=True),
        lax.all_gather(time_out_weight, "seq", axis=0, tiled=True),
        lax.all_gather(mix_weight, "seq", axis=0, tiled=True),
        lax.all_gather(time_mix_weight, "seq", axis=0, tiled=True),
        lax.all_gather(proj_weight, "seq", axis=0, tiled=True),
        lax.all_gather(up_weight, "seq", axis=0, tiled=True),
        lax.all_gather(down_weight, "seq", axis=0, tiled=True),
    )
    half_width = FREQ // 2
    frequency = jnp.exp(-math.log(10000.0) * jnp.arange(half_width, dtype=jnp.float32) / half_width)
    angles = timestep.astype(jnp.float32)[:, :, None] * frequency
    features = jnp.concatenate([jnp.cos(angles), jnp.sin(angles)], axis=-1).astype(jnp.bfloat16)
    time_pre = low_dot(features, full_tin) + time_in_bias
    time_hidden = jax.nn.silu(time_pre).astype(jnp.bfloat16)
    time_embed = (low_dot(time_hidden, full_tout) + time_out_bias).astype(jnp.bfloat16)
    time_proj = low_dot(time_embed, full_tmix)
    block_slots = image_ids[:, ::GRID]
    slot_hot = (block_slots[:, :, None] == jnp.arange(PACK, dtype=jnp.int32)[None, None, :]).astype(
        jnp.float32
    )
    unit_total = seq_rows * PACK
    unit_time = jnp.einsum("skp,spe->ske", slot_hot, time_proj, precision=highest).reshape(
        unit_total, 3 * D
    )
    act_tokens = tokens.reshape(seq_rows, local_rows, PACK, GRID, D)
    act_cot = cotangent.reshape(seq_rows, local_rows, PACK, GRID, D)
    act_time = unit_time.reshape(seq_rows, 1, PACK, 1, 3 * D)
    act_count, act_rows, act_slots = (act_tokens.shape[0], act_tokens.shape[1], act_tokens.shape[2])
    token_count = act_count * act_rows * act_slots * GRID
    flat_tokens = act_tokens.astype(jnp.float32)
    normed1, unit_one, inverse_one = norm_forward(flat_tokens, norm1_gain, norm1_shift)
    normed1 = normed1.astype(jnp.bfloat16)
    mixed_proj = low_dot(normed1, full_mix) + act_time
    queries = mixed_proj[..., :D].astype(jnp.bfloat16)
    key_rows = mixed_proj[..., D : 2 * D].astype(jnp.bfloat16)
    value_rows = mixed_proj[..., 2 * D :].astype(jnp.bfloat16)
    sent_rows = min(act_rows, REACH)
    turn_count = -(-REACH // act_rows)
    upper_keys, upper_values, lower_keys, lower_values = ([], [], [], [])
    for shift_turn in range(1, turn_count + 1):
        got_keys, got_values = passed_along(
            (key_rows[:, act_rows - sent_rows :], value_rows[:, act_rows - sent_rows :]),
            "rows",
            shift_turn,
        )
        upper_keys.insert(0, got_keys)
        upper_values.insert(0, got_values)
        got_keys, got_values = passed_along(
            (key_rows[:, :sent_rows], value_rows[:, :sent_rows]), "rows", -shift_turn
        )
        lower_keys.append(got_keys)
        lower_values.append(got_values)
    ext_keys = jnp.concatenate(upper_keys + [key_rows] + lower_keys, axis=1)
    ext_values = jnp.concatenate(upper_values + [value_rows] + lower_values, axis=1)
    margin = turn_count * sent_rows
    row_start = lax.axis_index("rows") * act_rows
    extent = act_rows + 2 * margin
    row_diff = jnp.arange(extent)[None, :] - margin - jnp.arange(act_rows)[:, None]
    row_global = row_start - margin + jnp.arange(extent)
    row_valid = (row_global >= 0) & (row_global < GRID)
    col_diff = jnp.arange(GRID)[None, :] - jnp.arange(GRID)[:, None]
    offsets = jnp.arange(2 * REACH + 1) - REACH
    row_hot = (row_diff[:, :, None] == offsets[None, None, :]).astype(jnp.float32)
    col_hot = (col_diff[:, :, None] == offsets[None, None, :]).astype(jnp.float32)
    col_hot_low = col_hot.astype(jnp.bfloat16)
    allowed = (
        (jnp.abs(row_diff) <= REACH)[:, None, :, None]
        & row_valid[None, None, :, None]
        & (jnp.abs(col_diff) <= REACH)[None, :, None, :]
    )
    bias_table = jnp.einsum(
        "hno,abn,ceo->hacbe", position_bias, row_hot, col_hot, precision=highest
    )
    group_size = math.gcd(act_count, max(1, 512 // (act_rows * act_slots * GRID)))
    blocks = act_count // group_size
    block_queries = queries.reshape(blocks, group_size, act_rows, act_slots, GRID, HEADS, HEAD_DIM)
    block_keys = ext_keys.reshape(blocks, group_size, extent, act_slots, GRID, HEADS, HEAD_DIM)
    block_values = ext_values.reshape(blocks, group_size, extent, act_slots, GRID, HEADS, HEAD_DIM)

    def score_block(block_q, block_k):
        scores = (
            jnp.einsum(
                "gakchd,gbkehd->gkhacbe", block_q, block_k, preferred_element_type=jnp.float32
            )
            * score_scale
            + bias_table
        )
        return jnp.where(allowed, scores, floor_score)

    def attend(inputs):
        block_q, block_k, block_v = inputs
        scores = score_block(block_q, block_k)
        row_top = jnp.max(scores, axis=(-2, -1), keepdims=True)
        row_total = jnp.sum(jnp.exp(scores - row_top), axis=(-2, -1), keepdims=True)
        log_total = row_top + jnp.log(row_total)
        probability = jnp.exp(scores - log_total).astype(jnp.bfloat16)
        result = jnp.einsum(
            "gkhacbe,gbkehd->gakchd", probability, block_v, preferred_element_type=jnp.float32
        )
        return (result.astype(jnp.bfloat16), log_total)

    attended, log_totals = lax.map(attend, (block_queries, block_keys, block_values))
    attended = attended.reshape(act_count, act_rows, act_slots, GRID, D)
    branch = low_dot(attended, full_proj) + proj_bias
    residual = flat_tokens + branch
    normed2, unit_two, inverse_two = norm_forward(residual, norm2_gain, norm2_shift)
    normed2 = normed2.astype(jnp.bfloat16)
    hidden_pre = low_dot(normed2, full_up) + up_bias
    hidden = gelu_tanh(hidden_pre).astype(jnp.bfloat16)
    output = (residual + low_dot(hidden, full_down) + down_bias).astype(jnp.bfloat16)
    flat_hidden = hidden.reshape(token_count, FF)
    flat_cot = act_cot.reshape(token_count, D)
    grad_down_w = jnp.einsum("nf,nd->fd", flat_hidden, flat_cot, preferred_element_type=jnp.float32)
    grad_down_b = jnp.sum(flat_cot, axis=0, dtype=jnp.float32)
    grad_hidden = jnp.einsum("nd,fd->nf", flat_cot, full_down, preferred_element_type=jnp.float32)
    gelu_back = jax.vjp(gelu_tanh, hidden_pre.reshape(token_count, FF))[1]
    grad_pre = gelu_back(grad_hidden)[0].astype(jnp.bfloat16)
    flat_normed2 = normed2.reshape(token_count, D)
    grad_up_w = jnp.einsum("nd,nf->df", flat_normed2, grad_pre, preferred_element_type=jnp.float32)
    grad_up_b = jnp.sum(grad_pre, axis=0, dtype=jnp.float32)
    grad_normed2 = jnp.einsum(
        "nf,df->nd", grad_pre, full_up, preferred_element_type=jnp.float32
    ).reshape(act_tokens.shape)
    grad_norm_two, grad_gain_two, grad_shift_two = norm_backward(
        grad_normed2, unit_two, inverse_two, norm2_gain
    )
    grad_residual = act_cot.astype(jnp.float32) + grad_norm_two
    grad_branch = grad_residual.astype(jnp.bfloat16).reshape(token_count, D)
    grad_proj_w = jnp.einsum(
        "nd,ne->de",
        attended.reshape(token_count, D),
        grad_branch,
        preferred_element_type=jnp.float32,
    )
    grad_proj_b = jnp.sum(grad_branch, axis=0, dtype=jnp.float32)
    grad_attended = jnp.einsum(
        "ne,de->nd", grad_branch, full_proj, preferred_element_type=jnp.float32
    ).astype(jnp.bfloat16)
    block_grads = grad_attended.reshape(
        blocks, group_size, act_rows, act_slots, GRID, HEADS, HEAD_DIM
    )

    def attend_back(inputs):
        block_q, block_k, block_v, log_total, block_g = inputs
        scores = score_block(block_q, block_k)
        probability = jnp.exp(scores - log_total)
        grad_v = jnp.einsum(
            "gkhacbe,gakchd->gbkehd",
            probability.astype(jnp.bfloat16),
            block_g,
            preferred_element_type=jnp.float32,
        )
        grad_prob = jnp.einsum(
            "gakchd,gbkehd->gkhacbe", block_g, block_v, preferred_element_type=jnp.float32
        )
        row_delta = jnp.sum(probability * grad_prob, axis=(-2, -1), keepdims=True)
        grad_scores = (probability * (grad_prob - row_delta)).astype(jnp.bfloat16)
        grad_q = (
            jnp.einsum(
                "gkhacbe,gbkehd->gakchd", grad_scores, block_k, preferred_element_type=jnp.float32
            )
            * score_scale
        )
        grad_k = (
            jnp.einsum(
                "gkhacbe,gakchd->gbkehd", grad_scores, block_q, preferred_element_type=jnp.float32
            )
            * score_scale
        )
        col_summed = jnp.einsum(
            "gkhacbe,ceo->habo", grad_scores, col_hot_low, preferred_element_type=jnp.float32
        )
        bias_part = jnp.einsum("habo,abn->hno", col_summed, row_hot, precision=highest)
        return (grad_q, grad_k, grad_v, bias_part)

    grad_q_all, grad_k_all, grad_v_all, bias_parts = lax.map(
        attend_back, (block_queries, block_keys, block_values, log_totals, block_grads)
    )
    grad_queries = grad_q_all.reshape(act_count, act_rows, act_slots, GRID, D)
    grad_keys = grad_k_all.reshape(act_count, extent, act_slots, GRID, D)
    grad_values = grad_v_all.reshape(act_count, extent, act_slots, GRID, D)
    own_keys = grad_keys[:, margin : margin + act_rows]
    own_values = grad_values[:, margin : margin + act_rows]
    for shift_turn in range(1, turn_count + 1):
        upper_at = (turn_count - shift_turn) * sent_rows
        back_keys, back_values = (
            passed_along(
                grad_keys[:, upper_at : upper_at + sent_rows].astype(jnp.bfloat16),
                "rows",
                -shift_turn,
            ).astype(jnp.float32),
            passed_along(
                grad_values[:, upper_at : upper_at + sent_rows].astype(jnp.bfloat16),
                "rows",
                -shift_turn,
            ).astype(jnp.float32),
        )
        own_keys = own_keys.at[:, act_rows - sent_rows :].add(back_keys)
        own_values = own_values.at[:, act_rows - sent_rows :].add(back_values)
        lower_at = margin + act_rows + (shift_turn - 1) * sent_rows
        back_keys, back_values = (
            passed_along(
                grad_keys[:, lower_at : lower_at + sent_rows].astype(jnp.bfloat16),
                "rows",
                shift_turn,
            ).astype(jnp.float32),
            passed_along(
                grad_values[:, lower_at : lower_at + sent_rows].astype(jnp.bfloat16),
                "rows",
                shift_turn,
            ).astype(jnp.float32),
        )
        own_keys = own_keys.at[:, :sent_rows].add(back_keys)
        own_values = own_values.at[:, :sent_rows].add(back_values)
    grad_mixed = jnp.concatenate([grad_queries, own_keys, own_values], axis=-1).astype(jnp.bfloat16)
    flat_mixed = grad_mixed.reshape(token_count, 3 * D)
    grad_mix_w = jnp.einsum(
        "nd,ne->de", normed1.reshape(token_count, D), flat_mixed, preferred_element_type=jnp.float32
    )
    grad_normed1 = jnp.einsum(
        "ne,de->nd", flat_mixed, full_mix, preferred_element_type=jnp.float32
    ).reshape(act_tokens.shape)
    unit_sum = jnp.sum(grad_mixed, axis=(1, 3), dtype=jnp.float32)
    grad_unit = unit_sum.reshape(unit_total, 3 * D)
    grad_time_proj = jnp.einsum(
        "skp,ske->spe", slot_hot, grad_unit.reshape(seq_rows, PACK, 3 * D), precision=highest
    )
    grad_tmix_w = jnp.einsum(
        "spd,spe->de", time_embed.astype(jnp.float32), grad_time_proj, precision=highest
    )
    grad_embed = jnp.einsum(
        "spe,de->spd", grad_time_proj, full_tmix.astype(jnp.float32), precision=highest
    )
    grad_tout_w = jnp.einsum(
        "spd,spe->de", time_hidden.astype(jnp.float32), grad_embed, precision=highest
    )
    grad_tout_b = jnp.sum(grad_embed, axis=(0, 1))
    grad_thidden = jnp.einsum(
        "spe,de->spd", grad_embed, full_tout.astype(jnp.float32), precision=highest
    )
    silu_back = jax.vjp(jax.nn.silu, time_pre)[1]
    grad_tpre = silu_back(grad_thidden)[0]
    grad_tin_w = jnp.einsum(
        "spf,spd->fd", features.astype(jnp.float32), grad_tpre, precision=highest
    )
    grad_tin_b = jnp.sum(grad_tpre, axis=(0, 1))
    grad_norm_one, grad_gain_one, grad_shift_one = norm_backward(
        grad_normed1, unit_one, inverse_one, norm1_gain
    )
    tokens_grad = (grad_residual + grad_norm_one).astype(jnp.bfloat16)
    bias_grad = jnp.sum(bias_parts, axis=0)
    weight_grads = (
        grad_tin_w,
        grad_tout_w,
        grad_mix_w,
        grad_tmix_w,
        grad_proj_w,
        grad_up_w,
        grad_down_w,
    )
    seq_parts = (
        lax.psum_scatter(
            weight_grads[0].astype(jnp.bfloat16), "seq", scatter_dimension=0, tiled=True
        ).astype(jnp.float32),
        lax.psum_scatter(
            weight_grads[1].astype(jnp.bfloat16), "seq", scatter_dimension=0, tiled=True
        ).astype(jnp.float32),
        lax.psum_scatter(
            weight_grads[2].astype(jnp.bfloat16), "seq", scatter_dimension=0, tiled=True
        ).astype(jnp.float32),
        lax.psum_scatter(
            weight_grads[3].astype(jnp.bfloat16), "seq", scatter_dimension=0, tiled=True
        ).astype(jnp.float32),
        lax.psum_scatter(
            weight_grads[4].astype(jnp.bfloat16), "seq", scatter_dimension=0, tiled=True
        ).astype(jnp.float32),
        lax.psum_scatter(
            weight_grads[5].astype(jnp.bfloat16), "seq", scatter_dimension=0, tiled=True
        ).astype(jnp.float32),
        lax.psum_scatter(
            weight_grads[6].astype(jnp.bfloat16), "seq", scatter_dimension=0, tiled=True
        ).astype(jnp.float32),
    )
    sum_tin, sum_tout, sum_mix, sum_tmix, sum_proj, sum_up, sum_down = (
        lax.psum(seq_parts[0].astype(jnp.bfloat16), "rows").astype(jnp.float32),
        lax.psum(seq_parts[1].astype(jnp.bfloat16), "rows").astype(jnp.float32),
        lax.psum(seq_parts[2].astype(jnp.bfloat16), "rows").astype(jnp.float32),
        lax.psum(seq_parts[3].astype(jnp.bfloat16), "rows").astype(jnp.float32),
        lax.psum(seq_parts[4].astype(jnp.bfloat16), "rows").astype(jnp.float32),
        lax.psum(seq_parts[5].astype(jnp.bfloat16), "rows").astype(jnp.float32),
        lax.psum(seq_parts[6].astype(jnp.bfloat16), "rows").astype(jnp.float32),
    )
    (
        gain_one,
        shift_one,
        tin_bias,
        tout_bias,
        bias_total,
        proj_total,
        gain_two,
        shift_two,
        up_total,
        down_total,
    ) = lax.psum(
        (
            grad_gain_one,
            grad_shift_one,
            grad_tin_b,
            grad_tout_b,
            bias_grad,
            grad_proj_b,
            grad_gain_two,
            grad_shift_two,
            grad_up_b,
            grad_down_b,
        ),
        ("seq", "rows"),
    )
    output = output.reshape(tokens.shape)
    tokens_grad = tokens_grad.reshape(tokens.shape)
    return (
        output,
        tokens_grad,
        gain_one,
        shift_one,
        sum_tin,
        tin_bias,
        sum_tout,
        tout_bias,
        sum_mix,
        sum_tmix,
        bias_total,
        sum_proj,
        proj_total,
        gain_two,
        shift_two,
        sum_up,
        up_total,
        sum_down,
        down_total,
    )


def solution(mesh):
    return jax.shard_map(
        on_device,
        mesh=mesh,
        in_specs=(
            P("seq", "rows", None, None),
            P("seq", None),
            P("seq", None),
            P(),
            P(),
            P("seq", None),
            P(),
            P("seq", None),
            P(),
            P("seq", None),
            P("seq", None),
            P(),
            P("seq", None),
            P(),
            P(),
            P(),
            P("seq", None),
            P(),
            P("seq", None),
            P(),
            P("seq", "rows", None, None),
        ),
        out_specs=(
            P("seq", "rows", None, None),
            P("seq", "rows", None, None),
            P(),
            P(),
            P("seq", None),
            P(),
            P("seq", None),
            P(),
            P("seq", None),
            P("seq", None),
            P(),
            P("seq", None),
            P(),
            P(),
            P(),
            P("seq", None),
            P(),
            P("seq", None),
            P(),
        ),
        check_vma=False,
    )
```

profile of v0, /device:TPU:0, one launch (start us, length us, event | category | flops | bytes accessed | tf_op | source)
XLA Modules:
  0.0 1989.2 jit_solution(6132097581884897629)
XLA Ops:
  15.4 25.4 %all_gather.22 = bf16[256,1152]{1,0:T(8,128)(2,1)S(1)} all-gather(bf16[16,1152]{1,0:T(8,128)(2,1)S(1)} %copy-done.44), channel_id=1, replica_groups=mesh['seq'=16,'rows'=2] {'seq'}, dimensions={0}, use_global_device_ids=true | all-gather | bytes 626688 | tf_op jit(solution)/shard_map/all_gather | solution.py:81
  41.3 9.7 convolution_bitcast_fusion.4
  51.0 17.8 copy.92
  71.5 59.4 %all-gather.11.cloned.1.call-done = bf16[1152,3456]{1,0:T(8,128)(2,1)} async-done(((bf16[72,3456]{1,0:T(8,128)(2,1)}), bf16[1152,3456]{1,0:T(8,128)(2,1)}) %all-gather.11.cloned.1.call-update) | async-done | bytes 7962640 | tf_op jit(solution)/shard_map/all_gather | solution.py:84
  135.8 67.9 %all-gather.7.cloned.1.call-done = bf16[1152,3456]{1,0:T(8,128)(2,1)} async-done(((bf16[72,3456]{1,0:T(8,128)(2,1)}), bf16[1152,3456]{1,0:T(8,128)(2,1)}) %all-gather.7.cloned.1.call-update) | async-done | bytes 7962640 | tf_op jit(solution)/shard_map/all_gather | solution.py:83
  203.7 12.7 add_convert_fusion
  224.8 7.9 collective-permute-start
  235.8 9.6 reshape.562
  253.2 24.3 %collective-permute-done.1 = bf16[2,4,4,16,1152]{4,3,2,1,0:T(8,128)(2,1)} collective-permute-done((bf16[2,4,4,16,1152]{4,3,2,1,0:T(8,128)(2,1)}, bf16[2,4,4,16,1152]{4,3,2,1,0:T(8,128)(2,1)}, u32[]{:S(2)}, u32[]{:S(2)}) %collective-permute-start.1) | collective-permute-done | bytes 1179680 | tf_op jit(solution)/shard_map/ppermute | solution.py:26
  283.6 17.4 reshape.561
  301.0 8.9 copy.89
  309.9 17.4 reshape.563
  327.3 9.1 copy.91
  336.5 203.3 %while.35 = (s32[]{:T(128)}, bf16[2,1,8,4,16,16,72]{6,5,4,3,2,0,1:T(8,128)(2,1)}, f32[2,1,4,16,8,16,1,1]{5,4,3,2,7,6,1,0:T(8,128)}, bf16[2,1,16,4,16,16,72]{6,4,...) while((s32[]{:T(128)}, ...), condition=%wide.region_5.6_spmd.clone, body=%wide.region_2.5_spmd.clone.sunk | while | flops 633954304 | bytes 135104000 | solution.py:182
  337.1 37.0 %fusion.195 = (f32[4,16,8,16]{3,2,1,0:T(8,128)S(1)}, f32[4,16,8,16,16,16]{3,5,4,2,1,0:T(8,128)}) fusion(f32[16,8,16,16,16]{2,4,3,1,0:T(8,128)} %get-tuple-element.701, pred[8,16,16,16]{1,3,2,0:T(8,128)(4,1)S(1)} %broadcast_and_fusion.4, bf16[2,1,16,4,16,16,72]{6,4,2,5,3,1,0:T(8,128)(2,1)} %get-tuple-element.700, s32[]{:T(128)S(6)} %copy.195, ...), kind=kOutput, calls=%fused_computation.7.clone.1 | convolution fusion | flops 310370304 | bytes 31523840 | tf_op jit(solution)/shard_map/while/body/eval_jaxpr/gakchd,gbkehd->gkhacbe/dot_general | solution.py:162
  374.1 28.0 %exponential_reduce_fusion.2 = f32[4,16,8,16]{3,2,1,0:T(8,128)S(1)} fusion(f32[4,16,8,16,16,16]{3,5,4,2,1,0:T(8,128)} %get-tuple-element.649, f32[4,16,8,16]{3,2,1,0:T(8,128)S(1)} %get-tuple-element.650, f32[16,8,16,16,16]{2,4,3,1,0:T(8,128)} %get-tuple-element.701, pred[8,16,16,16]{1,3,2,0:T(8,128)(4,1)S(1)} %broadcast_and_fusion.4), kind=kLoop, calls=%fused_computation.5.clone.1 | loop fusion | flops 10477568 | bytes 10584064 | tf_op jit(solution)/shard_map/while/body/eval_jaxpr/reduce_sum | solution.py:174
  402.8 32.9 %fusion.196 = bf16[1,1,8,4,16,16,72]{6,4,2,5,3,1,0:T(8,128)(2,1)S(1)} fusion(f32[4,16,8,16,16,16]{3,5,4,2,1,0:T(8,128)} %get-tuple-element.649, f32[4,16,8,16]{3,2,1,0:T(8,128)S(1)} %get-tuple-element.651, f32[16,8,16,16,16]{2,4,3,1,0:T(8,128)} %get-tuple-element.701, pred[8,16,16,16]{1,3,2,0:T(8,128)(4,1)S(1)} %broadcast_and_fusion.4, ...), kind=kOutput, calls=%fused_computation.16.clone.1 | convolution fusion | flops 313065472 | bytes 89325568 | tf_op jit(solution)/shard_map/while/body/eval_jaxpr/gkhacbe,gbkehd->gakchd/dot_general | solution.py:177
  439.7 36.9 %fusion.195 = (f32[4,16,8,16]{3,2,1,0:T(8,128)S(1)}, f32[4,16,8,16,16,16]{3,5,4,2,1,0:T(8,128)}) fusion(f32[16,8,16,16,16]{2,4,3,1,0:T(8,128)} %get-tuple-element.701, pred[8,16,16,16]{1,3,2,0:T(8,128)(4,1)S(1)} %broadcast_and_fusion.4, bf16[2,1,16,4,16,16,72]{6,4,2,5,3,1,0:T(8,128)(2,1)} %get-tuple-element.700, s32[]{:T(128)S(6)} %copy.195, ...), kind=kOutput, calls=%fused_computation.7.clone.1 | convolution fusion | flops 310370304 | bytes 31523840 | tf_op jit(solution)/shard_map/while/body/eval_jaxpr/gakchd,gbkehd->gkhacbe/dot_general | solution.py:162
  476.6 26.5 %exponential_reduce_fusion.2 = f32[4,16,8,16]{3,2,1,0:T(8,128)S(1)} fusion(f32[4,16,8,16,16,16]{3,5,4,2,1,0:T(8,128)} %get-tuple-element.649, f32[4,16,8,16]{3,2,1,0:T(8,128)S(1)} %get-tuple-element.650, f32[16,8,16,16,16]{2,4,3,1,0:T(8,128)} %get-tuple-element.701, pred[8,16,16,16]{1,3,2,0:T(8,128)(4,1)S(1)} %broadcast_and_fusion.4), kind=kLoop, calls=%fused_computation.5.clone.1 | loop fusion | flops 10477568 | bytes 10584064 | tf_op jit(solution)/shard_map/while/body/eval_jaxpr/reduce_sum | solution.py:174
  503.8 32.0 %fusion.196 = bf16[1,1,8,4,16,16,72]{6,4,2,5,3,1,0:T(8,128)(2,1)S(1)} fusion(f32[4,16,8,16,16,16]{3,5,4,2,1,0:T(8,128)} %get-tuple-element.649, f32[4,16,8,16]{3,2,1,0:T(8,128)S(1)} %get-tuple-element.651, f32[16,8,16,16,16]{2,4,3,1,0:T(8,128)} %get-tuple-element.701, pred[8,16,16,16]{1,3,2,0:T(8,128)(4,1)S(1)} %broadcast_and_fusion.4, ...), kind=kOutput, calls=%fused_computation.16.clone.1 | convolution fusion | flops 313065472 | bytes 89325568 | tf_op jit(solution)/shard_map/while/body/eval_jaxpr/gkhacbe,gbkehd->gakchd/dot_general | solution.py:177
  539.8 7.5 reshape_reshape.8
  547.3 7.7 reshape.564
  566.2 23.8 %fusion.73 = (bf16[2,8,4,16,4608]{4,3,2,1,0:T(8,128)(2,1)}, f32[2,8,4,16,4608]{4,3,2,1,0:T(8,128)}) fusion(f32[4608]{0:T(1024)S(1)} %copy-done.63, bf16[2,8,4,16,1152]{4,3,2,1,0:T(8,128)(2,1)} %add_convert_fusion.2, bf16[1152,4608]{1,0:T(8,128)(2,1)} %all-gather.15.cloned.1.call-done), kind=kOutput, calls=%fused_computation.91 | convolution fusion | flops 10918821888 | bytes 41306112 | tf_op jit(solution)/shard_map/dot_general | solution.py:30
  590.1 28.7 %convert_reduce_fusion.1 = (f32[4608]{0:T(1024)}, bf16[1024,4608]{1,0:T(8,128)(2,1)}) fusion(f32[2,8,4,16,4608]{4,3,2,1,0:T(8,128)} %get-tuple-element.494, bf16[1024,1152]{1,0:T(8,128)(2,1)S(1)} %bitcast.386, bf16[4608,1152]{1,0:T(8,128)(2,1)} %all-gather.17.cloned.1.call-done), kind=kOutput, calls=%fused_computation.95 | convolution fusion | flops 10975440896 | bytes 41306112 | tf_op jit(solution)/shard_map/nd,fd->nf/dot_general | solution.py:195
  618.8 20.2 %fusion.138 = (f32[1152]{0:T(1024)}, f32[1024]{0:T(1024)S(1)}, f32[1024,1152]{1,0:T(8,128)}) fusion(f32[1152]{0:T(1024)S(1)} %copy-done.40, bf16[1024,4608]{1,0:T(8,128)(2,1)} %get-tuple-element.468, bf16[1152,4608]{1,0:T(8,128)(2,1)} %all-gather.15.cloned.1.call-done), kind=kOutput, calls=%fused_computation.206 | convolution fusion | flops 10875172864 | bytes 24785920 | tf_op jit(solution)/shard_map/nf,df->nd/dot_general | solution.py:201
  639.1 7.1 multiply_reduce_fusion.1
  656.2 8.3 reshape.569
  664.6 507.9 %while.36 = (s32[]{:T(128)}, bf16[2,1,8,4,16,16,72]{6,4,2,5,3,1,0:T(8,128)(2,1)}, f32[2,1,16,4,16,16,72]{6,5,4,3,2,0,1:T(8,128)}, f32[2,1,16,4,16,16,72]{6,5,4,3...) while((s32[]{:T(128)}, ...), condition=%wide.region_13.14_spmd.clone.clone, body=%wide.region_10.13_spmd.clone.clone.sunk | while | flops 1547822080 | bytes 265184256 | solution.py:256
  686.2 25.3 %fusion.207 = f32[4,16,8,16,16,16]{3,5,4,2,1,0:T(8,128)} fusion(bf16[2,1,16,4,16,16,72]{6,4,2,5,3,1,0:T(8,128)(2,1)} %get-tuple-element.749, s32[]{:T(128)S(6)} %copy.206, bf16[1,1,8,4,16,16,72]{6,5,4,3,2,0,1:T(8,128)(2,1)S(1)} %constant_dynamic-slice_fusion.2), kind=kOutput, calls=%fused_computation.38.clone.1 | convolution fusion | flops 301989888 | bytes 13762564 | tf_op jit(solution)/shard_map/while/body/eval_jaxpr/gakchd,gbkehd->gkhacbe/dot_general | solution.py:233
  711.5 52.6 %multiply_reduce_fusion.10 = (f32[4,16,8,16]{3,2,1,0:T(8,128)S(1)}, f32[4,16,8,16,16,16]{3,5,4,2,1,0:T(8,128)}) fusion(f32[4,16,8,16,16,16]{3,5,4,2,1,0:T(8,128)} %fusion.207, f32[4,16,8,16]{3,2,1,0:T(8,128)S(1)} %dynamic-slice_bitcast_fusion.2, f32[16,8,16,16,16]{2,4,3,1,0:T(8,128)} %get-tuple-element.746, ...), kind=kOutput, calls=%fused_computation.29.clone.3 | convolution fusion | flops 314564608 | bytes 98665472 | tf_op jit(solution)/shard_map/while/body/eval_jaxpr/gakchd,gbkehd->gkhacbe/dot_general | solution.py:162
  764.1 57.7 %convert_reduce_fusion.7 = (bf16[16,8,16,16,16]{2,4,3,1,0:T(8,128)(2,1)}, bf16[4,16,8,16,16,16]{3,5,4,2,1,0:T(8,128)(2,1)}) fusion(f32[4,16,8,16,16,16]{3,5,4,2,1,0:T(8,128)} %get-tuple-element.669, f32[4,16,8,16,16,16]{3,5,4,2,1,0:T(8,128)} %fusion.207, f32[4,16,8,16]{3,2,1,0:T(8,128)S(1)} %get-tuple-element.670), kind=kLoop, calls=%fused_computation.27.clone.1 | loop fusion | flops 9961472 | bytes 22052864 | tf_op jit(solution)/shard_map/while/body/eval_jaxpr/gkhacbe,ceo->habo/reduce_sum | solution.py:250
  821.8 26.0 %fusion.208 = f32[1,1,16,4,16,16,72]{6,4,2,5,3,1,0:T(8,128)} fusion(f32[4,16,8,16,16,16]{3,5,4,2,1,0:T(8,128)} %get-tuple-element.669, bf16[1,1,8,4,16,16,72]{6,5,4,3,2,0,1:T(8,128)(2,1)S(1)} %constant_dynamic-slice_fusion.2), kind=kOutput, calls=%fused_computation.47.clone.1 | convolution fusion | flops 304087040 | bytes 14286848 | tf_op jit(solution)/shard_map/while/body/eval_jaxpr/gkhacbe,gakchd->gbkehd/dot_general | solution.py:227
  847.8 13.0 copy.185
  860.9 13.5 convolution_bitcast_fusion.8
  875.5 16.6 bitcast_dynamic-update-slice_fusion.7
  892.1 15.1 fusion.209
  907.2 16.2 copy_dynamic-update-slice_fusion.6
  927.2 25.3 %fusion.207 = f32[4,16,8,16,16,16]{3,5,4,2,1,0:T(8,128)} fusion(bf16[2,1,16,4,16,16,72]{6,4,2,5,3,1,0:T(8,128)(2,1)} %get-tuple-element.749, s32[]{:T(128)S(6)} %copy.206, bf16[1,1,8,4,16,16,72]{6,5,4,3,2,0,1:T(8,128)(2,1)S(1)} %constant_dynamic-slice_fusion.2), kind=kOutput, calls=%fused_computation.38.clone.1 | convolution fusion | flops 301989888 | bytes 13762564 | tf_op jit(solution)/shard_map/while/body/eval_jaxpr/gakchd,gbkehd->gkhacbe/dot_general | solution.py:233
  952.5 52.6 %multiply_reduce_fusion.10 = (f32[4,16,8,16]{3,2,1,0:T(8,128)S(1)}, f32[4,16,8,16,16,16]{3,5,4,2,1,0:T(8,128)}) fusion(f32[4,16,8,16,16,16]{3,5,4,2,1,0:T(8,128)} %fusion.207, f32[4,16,8,16]{3,2,1,0:T(8,128)S(1)} %dynamic-slice_bitcast_fusion.2, f32[16,8,16,16,16]{2,4,3,1,0:T(8,128)} %get-tuple-element.746, ...), kind=kOutput, calls=%fused_computation.29.clone.3 | convolution fusion | flops 314564608 | bytes 98665472 | tf_op jit(solution)/shard_map/while/body/eval_jaxpr/gakchd,gbkehd->gkhacbe/dot_general | solution.py:162
  1005.1 57.7 %convert_reduce_fusion.7 = (bf16[16,8,16,16,16]{2,4,3,1,0:T(8,128)(2,1)}, bf16[4,16,8,16,16,16]{3,5,4,2,1,0:T(8,128)(2,1)}) fusion(f32[4,16,8,16,16,16]{3,5,4,2,1,0:T(8,128)} %get-tuple-element.669, f32[4,16,8,16,16,16]{3,5,4,2,1,0:T(8,128)} %fusion.207, f32[4,16,8,16]{3,2,1,0:T(8,128)S(1)} %get-tuple-element.670), kind=kLoop, calls=%fused_computation.27.clone.1 | loop fusion | flops 9961472 | bytes 22052864 | tf_op jit(solution)/shard_map/while/body/eval_jaxpr/gkhacbe,ceo->habo/reduce_sum | solution.py:250
  1062.8 26.0 %fusion.208 = f32[1,1,16,4,16,16,72]{6,4,2,5,3,1,0:T(8,128)} fusion(f32[4,16,8,16,16,16]{3,5,4,2,1,0:T(8,128)} %get-tuple-element.669, bf16[1,1,8,4,16,16,72]{6,5,4,3,2,0,1:T(8,128)(2,1)S(1)} %constant_dynamic-slice_fusion.2), kind=kOutput, calls=%fused_computation.47.clone.1 | convolution fusion | flops 304087040 | bytes 14286848 | tf_op jit(solution)/shard_map/while/body/eval_jaxpr/gkhacbe,gakchd->gbkehd/dot_general | solution.py:227
  1088.9 13.0 copy.185
  1101.9 13.5 convolution_bitcast_fusion.8
  1116.5 16.6 bitcast_dynamic-update-slice_fusion.7
  1133.1 15.1 fusion.209
  1148.2 16.2 copy_dynamic-update-slice_fusion.6
  1172.5 15.7 reshape.570
  1194.7 15.7 reshape.571
  1227.3 9.0 copy.101
  1256.9 18.7 collective-permute-done.5
  1281.7 16.8 collective-permute-done.7
  1313.4 14.9 fusion.76
  1329.0 8.5 fusion.77
  1337.6 18.6 convolution_convert_fusion
  1356.3 17.0 convolution_convert_fusion.1
  1381.3 20.3 %fusion.95 = bf16[2,8,4,16,1152]{4,3,2,1,0:T(8,128)(2,1)} fusion(f32[2,8,4,16,1152]{4,3,2,1,0:T(8,128)} %copy-done, bf16[2,8,4,16,4608]{4,3,2,1,0:T(8,128)(2,1)} %get-tuple-element.493, bf16[4608,1152]{1,0:T(8,128)(2,1)} %all-gather.17.cloned.1.call-done, f32[1152]{0:T(1024)S(1)} %copy-done.67), kind=kOutput, calls=%fused_computation.138 | convolution fusion | flops 10875174912 | bytes 27136512 | tf_op jit(solution)/shard_map/dot_general | solution.py:30
  1401.7 79.0 %reduce-scatter.24.cloned.1.call-done = bf16[72,3456]{1,0:T(8,128)(2,1)} async-done(((bf16[1152,3456]{1,0:T(8,128)(2,1)}), bf16[72,3456]{1,0:T(8,128)(2,1)}) %reduce-scatter.24.cloned.1.call-update) | async-done | bytes 497680
  1480.6 105.2 %reduce-scatter.26.cloned.1.call-done = bf16[72,3456]{1,0:T(8,128)(2,1)} async-done(((bf16[1152,3456]{1,0:T(8,128)(2,1)}), bf16[72,3456]{1,0:T(8,128)(2,1)}) %reduce-scatter.26.cloned.1.call-update) | async-done | bytes 497680
  1585.8 124.1 %reduce-scatter.20.cloned.1.call-done = bf16[288,1152]{1,0:T(8,128)(2,1)} async-done(((bf16[4608,1152]{1,0:T(8,128)(2,1)}), bf16[288,1152]{1,0:T(8,128)(2,1)}) %reduce-scatter.20.cloned.1.call-update) | async-done | bytes 663568 | tf_op jit(solution)/shard_map/reduce_scatter | solution.py:360
  1709.9 123.9 %reduce-scatter.18.cloned.1.call-done = bf16[72,4608]{1,0:T(8,128)(2,1)} async-done(((bf16[1152,4608]{1,0:T(8,128)(2,1)}), bf16[72,4608]{1,0:T(8,128)(2,1)}) %reduce-scatter.18.cloned.1.call-update) | async-done | bytes 663568 | tf_op jit(solution)/shard_map/reduce_scatter | solution.py:357
  1833.9 15.9 multiply_reduce_fusion.2
  1849.9 44.5 %all-reduce.4 = (f32[1152]{0:T(1024)}, f32[1152]{0:T(1024)}, f32[1152]{0:T(1024)}, f32[1152]{0:T(1024)}, f32[16,9,9]{1,0,2:T(8,128)S(1)}, /*index=5*/f32[1152]{0...) all-reduce(f32[1152]{0:T(1024)S(1)} %get-tuple-element.389, ...), channel_id=1, replica_groups=mesh['seq'=16,'rows'=2] {'seq','rows'}, use_global_device_ids=true, to_apply=%region_17.18 | all-reduce | flops 15120 | bytes 120960 | tf_op jit(solution)/shard_map/psum | solution.py:384
  1900.8 10.0 psum.121
  1911.5 59.8 %all-reduce.8.cloned.1.call-done = (bf16[72,1152]{1,0:T(8,128)(2,1)}, bf16[72,3456]{1,0:T(8,128)(2,1)}, bf16[72,3456]{1,0:T(8,128)(2,1)}, bf16[72,1152]{1,0:T(8,...) async-done(((bf16[72,1152]{1,0:T(8,128)(2,1)}, bf16[72,3456]{1,0:T(8,128)(2,1)}, bf16[72,3456]{1,0:T(8,128)(2,1)}, bf16[72,1152]{1,0:T(8,128)(2,1)}, ...) | async-done | bytes 2654224 | tf_op jit(solution)/shard_map/psum | solution.py:366
  (302 shorter events, 173.0 us)
Async XLA Ops:
  7.2 62.0 %all-gather.9.cloned.1.call-start = ((), (), s32[]{:S(2)}) async-start(), calls=%async_computation.8 | async-start | bytes 2820096 | tf_op jit(solution)/shard_map/all_gather | solution.py:82
  8.0 123.0 %all-gather.11.cloned.1.call-start = ((), (), s32[]{:S(2)}) async-start(), calls=%async_computation.9 | async-start | bytes 8460288 | tf_op jit(solution)/shard_map/all_gather | solution.py:84
  8.7 195.0 %all-gather.7.cloned.1.call-start = ((), (), s32[]{:S(2)}) async-start(), calls=%async_computation.7 | async-start | bytes 8460288 | tf_op jit(solution)/shard_map/all_gather | solution.py:83
  9.5 545.5 %all-gather.13.cloned.1.call-start = ((), (), s32[]{:S(2)}) async-start(), calls=%async_computation.10 | async-start | bytes 2820096 | tf_op jit(solution)/shard_map/all_gather | solution.py:85
  10.0 556.2 %all-gather.15.cloned.1.call-start = ((), (), s32[]{:S(2)}) async-start(), calls=%async_computation.11 | async-start | bytes 11280384 | tf_op jit(solution)/shard_map/all_gather | solution.py:86
  10.6 579.5 %all-gather.17.cloned.1.call-start = ((), (), s32[]{:S(2)}) async-start(), calls=%async_computation.12 | async-start | bytes 11280384 | tf_op jit(solution)/shard_map/all_gather | solution.py:87
  11.2 1390.4 %reduce-scatter.28.cloned.1.call-start = ((), (), s32[]{:S(2)}) async-start(), calls=%async_computation.19 | async-start | bytes 2820096
  11.3 39.7 %copy-start.41 = (s32[9]{0:T(128)}, s32[9]{0:T(128)S(1)}, u32[]{:S(2)}) copy-start(s32[9]{0:T(128)S(1)} %iota_add_fusion) | copy-start | bytes 112
  11.3 39.7 %copy-start.22 = (s32[16,16]{1,0:T(8,128)}, s32[16,16]{1,0:T(8,128)S(1)}, u32[]{:S(2)}) copy-start(s32[16,16]{1,0:T(8,128)S(1)} %iota_subtract_fusion) | copy-start | bytes 3076
  14.3 189.4 %copy-start.32 = (f32[2,8,4,16]{3,2,1,0:T(4,128)}, f32[2,8,4,16]{3,2,1,0:T(4,128)S(1)}, u32[]{:S(2)}) copy-start(f32[2,8,4,16]{3,2,1,0:T(4,128)S(1)} %div.41) | copy-start | bytes 12292
  14.4 121.0 %copy-start.52 = (s32[2,4]{1,0:T(2,128)}, s32[2,4]{1,0:T(2,128)S(1)}, u32[]{:S(2)}) copy-start(s32[2,4]{1,0:T(2,128)S(1)} %slice.191) | copy-start | bytes 100
  15.1 35.9 %copy-start.27 = (s32[8,16]{1,0:T(8,128)}, s32[8,16]{1,0:T(8,128)S(1)}, u32[]{:S(2)}) copy-start(s32[8,16]{1,0:T(8,128)S(1)} %iota_subtract_fusion.1) | copy-start | bytes 1540
  15.2 188.5 %copy-start.34 = (f32[2,8,4,16]{3,2,1,0:T(4,128)}, f32[2,8,4,16]{3,2,1,0:T(4,128)S(1)}, u32[]{:S(2)}) copy-start(f32[2,8,4,16]{3,2,1,0:T(4,128)S(1)} %rsqrt.20) | copy-start | bytes 12292
  51.0 18.0 copy-start.54
  51.0 18.2 copy-start.55
  69.0 66.5 %copy-start.48 = (bf16[2,4,128]{2,1,0:T(4,128)(2,1)}, bf16[2,4,128]{2,1,0:T(4,128)(2,1)S(1)}, u32[]{:S(2)}) copy-start(bf16[2,4,128]{2,1,0:T(4,128)(2,1)S(1)} %get-tuple-element.489) | copy-start | bytes 6148
  69.0 66.5 %copy-start.50 = (bf16[2,4,128]{2,1,0:T(4,128)(2,1)}, bf16[2,4,128]{2,1,0:T(4,128)(2,1)S(1)}, u32[]{:S(2)}) copy-start(bf16[2,4,128]{2,1,0:T(4,128)(2,1)S(1)} %get-tuple-element.490) | copy-start | bytes 6148
  69.2 66.2 %copy-start.18 = (f32[2,4,1152]{2,1,0:T(4,128)}, f32[2,4,1152]{2,1,0:T(4,128)S(1)}, u32[]{:S(2)}) copy-start(f32[2,4,1152]{2,1,0:T(4,128)S(1)} %convolution_add_fusion.1) | copy-start | bytes 110596
  71.5 64.0 %copy-start.25 = (bf16[2,4,1152]{2,1,0:T(4,128)(2,1)}, bf16[2,4,1152]{2,1,0:T(4,128)(2,1)S(1)}, u32[]{:S(2)}) copy-start(bf16[2,4,1152]{2,1,0:T(4,128)(2,1)S(1)} %fusion.111) | copy-start | bytes 55300
  71.5 132.2 %copy-start.57 = (f32[1152]{0:T(1024)S(1)}, f32[1152]{0:T(1024)}, u32[]{:S(2)}) copy-start(f32[1152]{0:T(1024)} %param.36) | copy-start | bytes 13828
  71.5 132.2 %copy-start.65 = (f32[1152]{0:T(1024)S(1)}, f32[1152]{0:T(1024)}, u32[]{:S(2)}) copy-start(f32[1152]{0:T(1024)} %param.37) | copy-start | bytes 13828
  218.7 32.2 %collective-permute-start.2 = (bf16[2,4,4,16,1152]{4,3,2,1,0:T(8,128)(2,1)}, bf16[2,4,4,16,1152]{4,3,2,1,0:T(8,128)(2,1)S(1)}, u32[]{:S(2)}, u32[]{:S(2)}) collective-permute-start(bf16[2,4,4,16,1152]{4,3,2,1,0:T(8,128)(2,1)} %get-tuple-element.478), channel_id=1, source_target_pairs={{0,1},{2,3},{4,5},{6,7},{8,9},{10,11},{12,13},{14,15},{16,17},{18,... | collective-permute-start | bytes 3538952 | tf_op jit(solution)/shard_map/ppermute | solution.py:26
  222.2 31.0 %collective-permute-start.3 = (bf16[2,4,4,16,1152]{4,3,2,1,0:T(8,128)(2,1)}, bf16[2,4,4,16,1152]{4,3,2,1,0:T(8,128)(2,1)}, u32[]{:S(2)}, u32[]{:S(2)}) collective-permute-start(bf16[2,4,4,16,1152]{4,3,2,1,0:T(8,128)(2,1)} %get-tuple-element.479), channel_id=1, source_target_pairs={{1,0},{3,2},{5,4},{7,6},{9,8},{11,10},{13,12},{15,14},{17,16},{19,... | collective-permute-start | bytes 3538952 | tf_op jit(solution)/shard_map/ppermute | solution.py:26
  223.5 54.0 %collective-permute-start.1 = (bf16[2,4,4,16,1152]{4,3,2,1,0:T(8,128)(2,1)}, bf16[2,4,4,16,1152]{4,3,2,1,0:T(8,128)(2,1)}, u32[]{:S(2)}, u32[]{:S(2)}) collective-permute-start(bf16[2,4,4,16,1152]{4,3,2,1,0:T(8,128)(2,1)} %get-tuple-element.480), channel_id=1, source_target_pairs={{1,0},{3,2},{5,4},{7,6},{9,8},{11,10},{13,12},{15,14},{17,16},{19,... | collective-permute-start | bytes 3538952 | tf_op jit(solution)/shard_map/ppermute | solution.py:26
  224.8 52.7 %collective-permute-start = (bf16[2,4,4,16,1152]{4,3,2,1,0:T(8,128)(2,1)}, bf16[2,4,4,16,1152]{4,3,2,1,0:T(8,128)(2,1)}, u32[]{:S(2)}, u32[]{:S(2)}) collective-permute-start(bf16[2,4,4,16,1152]{4,3,2,1,0:T(8,128)(2,1)} %get-tuple-element.481), channel_id=1, source_target_pairs={{0,1},{2,3},{4,5},{6,7},{8,9},{10,11},{12,13},{14,15},{16,17},{18,... | collective-permute-start | bytes 3538952 | tf_op jit(solution)/shard_map/ppermute | solution.py:26
  245.5 32.0 %copy-start.7 = (bf16[2,8,4,16,1152]{4,3,2,1,0:T(8,128)(2,1)S(1)}, bf16[2,8,4,16,1152]{4,3,2,1,0:T(8,128)(2,1)}, u32[]{:S(2)}) copy-start(bf16[2,8,4,16,1152]{4,3,2,1,0:T(8,128)(2,1)} %get-tuple-element.484) | copy-start | bytes 7077892
  539.8 15.2 copy-start.36
  566.2 23.8 %copy-start.11 = (bf16[2,8,64,1152]{3,2,1,0:T(8,128)(2,1)S(1)}, bf16[2,8,64,1152]{3,2,1,0:T(8,128)(2,1)}, u32[]{:S(2)}) copy-start(bf16[2,8,64,1152]{3,2,1,0:T(8,128)(2,1)} %param.53) | copy-start | bytes 7077892
  590.1 28.7 %copy-start.40 = (f32[1152]{0:T(1024)S(1)}, f32[1152]{0:T(1024)}, u32[]{:S(2)}) copy-start(f32[1152]{0:T(1024)} %param.47) | copy-start | bytes 13828
  618.8 20.3 %copy-start.16 = (f32[2,8,4,16]{3,2,1,0:T(4,128)S(1)}, f32[2,8,4,16]{3,2,1,0:T(4,128)}, u32[]{:S(2)}) copy-start(f32[2,8,4,16]{3,2,1,0:T(4,128)} %copy-done.15) | copy-start | bytes 12292
  618.8 20.3 %copy-start.21 = (f32[2,8,4,16]{3,2,1,0:T(4,128)S(1)}, f32[2,8,4,16]{3,2,1,0:T(4,128)}, u32[]{:S(2)}) copy-start(f32[2,8,4,16]{3,2,1,0:T(4,128)} %copy-done.20) | copy-start | bytes 12292
  847.8 13.0 copy-start.23
  847.8 13.0 copy-start.42
  860.9 13.5 copy-start.28
  860.9 14.5 copy-start.29
  875.4 16.6 copy-start.30
  907.2 16.2 copy-start.38
  1088.8 13.0 copy-start.23
  1088.9 13.0 copy-start.42
  1101.9 13.5 copy-start.28
  1101.9 14.5 copy-start.29
  1116.5 16.6 copy-start.30
  1148.2 16.2 copy-start.38
  1220.8 33.4 %collective-permute-start.4 = (bf16[2,4,4,16,1152]{4,3,2,1,0:T(8,128)(2,1)}, bf16[2,4,4,16,1152]{4,3,2,1,0:T(8,128)(2,1)}, u32[]{:S(2)}, u32[]{:S(2)}) collective-permute-start(bf16[2,4,4,16,1152]{4,3,2,1,0:T(8,128)(2,1)} %get-tuple-element.486), channel_id=1, source_target_pairs={{1,0},{3,2},{5,4},{7,6},{9,8},{11,10},{13,12},{15,14},{17,16},{19,... | collective-permute-start | bytes 3538952 | tf_op jit(solution)/shard_map/ppermute | solution.py:26
  1227.2 174.4 %reduce-scatter.22.cloned.1.call-start = ((), (), s32[]{:S(2)}) async-start(), calls=%async_computation.16 | async-start | bytes 2820096
  1236.3 45.1 %slice-start = ((s8[9437184]{0:T(1024)(128)(4,1)}), s8[1048576]{0:T(1024)(128)(4,1)S(1)}, s32[]{:S(2)}) async-start(s8[9437184]{0:T(1024)(128)(4,1)} %bitcast.376), calls=%async_computation.21 | async-start | bytes 2097152
  1243.2 56.2 %copy-start.8 = (bf16[2,8,4,16,1152]{4,3,2,1,0:T(8,128)(2,1)}, bf16[2,8,4,16,1152]{4,3,2,1,0:T(8,128)(2,1)S(1)}, u32[]{:S(2)}) copy-start(bf16[2,8,4,16,1152]{4,3,2,1,0:T(8,128)(2,1)S(1)} %concatenate.29) | copy-start | bytes 7077892
  1243.2 38.2 %slice-start.1 = ((s8[9437184]{0:T(1024)(128)(4,1)}), s8[4194304]{0:T(1024)(128)(4,1)S(1)}, s32[]{:S(2)}) async-start(s8[9437184]{0:T(1024)(128)(4,1)} %bitcast.376), calls=%async_computation.22 | async-start | bytes 8388608
  1243.2 32.4 %collective-permute-start.5 = (bf16[2,4,4,16,1152]{4,3,2,1,0:T(8,128)(2,1)}, bf16[2,4,4,16,1152]{4,3,2,1,0:T(8,128)(2,1)S(1)}, u32[]{:S(2)}, u32[]{:S(2)}) collective-permute-start(bf16[2,4,4,16,1152]{4,3,2,1,0:T(8,128)(2,1)} %get-tuple-element.485), channel_id=1, source_target_pairs={{0,1},{2,3},{4,5},{6,7},{8,9},{10,11},{12,13},{14,15},{16,17},{18,... | collective-permute-start | bytes 3538952 | tf_op jit(solution)/shard_map/ppermute | solution.py:26
  1250.8 47.7 %collective-permute-start.7 = (bf16[2,4,4,16,1152]{4,3,2,1,0:T(8,128)(2,1)S(1)}, bf16[2,4,4,16,1152]{4,3,2,1,0:T(8,128)(2,1)S(1)}, u32[]{:S(2)}, u32[]{:S(2)}) collective-permute-start(bf16[2,4,4,16,1152]{4,3,2,1,0:T(8,128)(2,1)S(1)} %get-tuple-element.487), channel_id=1, source_target_pairs={{0,1},{2,3},{4,5},{6,7},{8,9},{10,11},{12,13},{14,15},{16,17},{18,... | collective-permute-start | bytes 3538952 | tf_op jit(solution)/shard_map/ppermute | solution.py:26
  1253.0 28.4 %collective-permute-start.6 = (bf16[2,4,4,16,1152]{4,3,2,1,0:T(8,128)(2,1)S(1)}, bf16[2,4,4,16,1152]{4,3,2,1,0:T(8,128)(2,1)S(1)}, u32[]{:S(2)}, u32[]{:S(2)}) collective-permute-start(bf16[2,4,4,16,1152]{4,3,2,1,0:T(8,128)(2,1)S(1)} %get-tuple-element.488), channel_id=1, source_target_pairs={{1,0},{3,2},{5,4},{7,6},{9,8},{11,10},{13,12},{15,14},{17,16},{19,... | collective-permute-start | bytes 3538952 | tf_op jit(solution)/shard_map/ppermute | solution.py:26
  1256.9 24.5 %slice-start.2 = ((s8[9437184]{0:T(1024)(128)(4,1)}), s8[4194304]{0:T(1024)(128)(4,1)S(1)}, s32[]{:S(2)}) async-start(s8[9437184]{0:T(1024)(128)(4,1)} %bitcast.376), calls=%async_computation.23 | async-start | bytes 8388608
  1276.6 22.9 %copy-start.9 = (bf16[2,8,4,16,1152]{4,3,2,1,0:T(8,128)(2,1)}, bf16[2,8,4,16,1152]{4,3,2,1,0:T(8,128)(2,1)S(1)}, u32[]{:S(2)}) copy-start(bf16[2,8,4,16,1152]{4,3,2,1,0:T(8,128)(2,1)S(1)} %convert.36) | copy-start | bytes 7077892
  1313.3 167.4 %reduce-scatter.24.cloned.1.call-start = ((), (), s32[]{:S(2)}) async-start(), calls=%async_computation.17 | async-start | bytes 8460288
  1328.3 257.5 %reduce-scatter.26.cloned.1.call-start = ((), (), s32[]{:S(2)}) async-start(), calls=%async_computation.18 | async-start | bytes 8460288
  1337.5 372.4 %reduce-scatter.20.cloned.1.call-start = ((), (), s32[]{:S(2)}) async-start(), calls=%async_computation.15 | async-start | bytes 11280384 | tf_op jit(solution)/shard_map/reduce_scatter | solution.py:360
  1356.2 477.6 %reduce-scatter.18.cloned.1.call-start = ((), (), s32[]{:S(2)}) async-start(), calls=%async_computation.14 | async-start | bytes 11280384 | tf_op jit(solution)/shard_map/reduce_scatter | solution.py:357
  1373.4 527.5 %reduce-scatter.16.cloned.1.call-start = ((), (), s32[]{:S(2)}) async-start(), calls=%async_computation.13 | async-start | bytes 626688 | tf_op jit(solution)/shard_map/reduce_scatter | solution.py:342
  1381.3 20.3 %copy-start.31 = (f32[2,16,9,9]{2,1,3,0:T(8,128)S(1)}, f32[2,16,9,9]{2,1,3,0:T(8,128)}, u32[]{:S(2)}) copy-start(f32[2,16,9,9]{2,1,3,0:T(8,128)} %get-tuple-element.846) | copy-start | bytes 31108
  1381.3 590.0 %all-reduce.8.cloned.1.call-start = ((), (), s32[]{:S(2)}) async-start(), calls=%async_computation.20 | async-start | bytes 5308416 | tf_op jit(solution)/shard_map/psum | solution.py:366
  1833.9 15.9 copy-start.45
  1833.9 15.9 copy-start.46
  1833.9 15.9 copy-start.47
  1833.9 15.9 copy-start.59
  (39 other events, 207.9 us)
Sparse Core Ops, SparseCore 0:
  10.2 47.6 all-gather.8
  60.1 70.8 all-gather.10
  133.1 70.5 all-gather.6
  205.7 41.6 all-gather.12
  249.5 87.3 all-gather.14
  339.1 86.8 all-gather.16
  1227.4 64.3 reduce-scatter.27
  1313.4 63.3 reduce-scatter.21
  1380.9 99.6 reduce-scatter.23
  1485.1 100.6 reduce-scatter.25
  1589.9 120.0 reduce-scatter.19
  1713.9 119.9 reduce-scatter.17
  1838.0 54.6 reduce-scatter.15
  1895.4 75.8 all-reduce.7
where the time goes:
time: 2000 us; the launch traced here: 1990 us
  waiting for transfers between devices  690 us (34%)
  matrix products  668 us (33%)
  local copies, waits for them, and re-layouts  249 us (12%)
  other arithmetic  235 us (12%)
  blocking collectives  79.9 us (4%)
  loops' own time  26.6 us (1%)
  starting transfers between devices  25.3 us (1%)
    unnamed x18, waiting for transfers between devices  188 us
    dot_general x4, matrix products, score_block(): jnp.einsum('gakchd,gbkehd->gkhacbe', block_q, block_k, preferred_element_...  179 us
    reduce_scatter x1, waiting for transfers between devices, on_device(): lax.psum_scatter(weight_grads[6].astype(jnp.bfloat16), 'seq', scatter_dim...  124 us
    reduce_scatter x1, waiting for transfers between devices, on_device(): lax.psum_scatter(weight_grads[5].astype(jnp.bfloat16), 'seq', scatter_dim...  124 us
    reduce_sum x2, other arithmetic, attend_back(): jnp.einsum('gkhacbe,ceo->habo', grad_scores, col_hot_low, preferred_eleme...  115 us
    dot_general x7, matrix products, low_dot(): return jnp.dot(left, right, preferred_element_type=jnp.float32)  69.8 us
    all_gather x1, waiting for transfers between devices, on_device(): lax.all_gather(mix_weight, 'seq', axis=0, tiled=True)  67.9 us
    ppermute x8, waiting for transfers between devices, passed_along(): return lax.ppermute(block, axis, route)  66.9 us
  transfers between devices with their start and end apart: 22, of which 12 were waited for; matrix products, arithmetic and copies ran while one was open for 27% of the time, Pallas kernels for 0%

commit v1 on v0

v1 whole, which is shorter than its diff:
```python
import functools
import math

import jax
import jax.numpy as jnp
from jax import lax
from jax.experimental import pallas as pl
from jax.experimental.pallas import tpu as pltpu
from jax.sharding import PartitionSpec as P

D = 1152
HEADS = 16
HEAD_DIM = 72
FF = 4608
FREQ = 256
GRID = 16
PACK = 4
REACH = 4
LANES = 128


epsilon = 1e-06
floor_score = -1e30
highest = lax.Precision.HIGHEST
score_scale = HEAD_DIM ** (-0.5)


def low_dot(left, right):
    return jnp.dot(left, right, preferred_element_type=jnp.float32)


def gelu_tanh(values):
    return jax.nn.gelu(values, approximate=True)


def norm_forward(values, norm_gain, norm_shift):
    centred = values - jnp.mean(values, axis=-1, keepdims=True)
    inverse = lax.rsqrt(jnp.mean(centred * centred, axis=-1, keepdims=True) + epsilon)
    unit_rows = centred * inverse
    return (unit_rows * norm_gain + norm_shift, unit_rows, inverse)


def norm_backward(grad_out, unit_rows, inverse, norm_gain):
    scaled = grad_out * norm_gain
    grad_in = inverse * (
        scaled
        - jnp.mean(scaled, axis=-1, keepdims=True)
        - unit_rows * jnp.mean(scaled * unit_rows, axis=-1, keepdims=True)
    )
    leading = tuple(range(grad_out.ndim - 1))
    return (grad_in, jnp.sum(grad_out * unit_rows, axis=leading), jnp.sum(grad_out, axis=leading))


def row_plan(local_rows, shards):
    if shards == 2 and local_rows >= REACH:
        return (True, 1, REACH)
    sent = min(local_rows, REACH)
    return (False, -(-REACH // local_rows), sent)


def route(shards, distance):
    return [(i - distance, i) for i in range(shards) if 0 <= i - distance < shards]


def borrow_rows(own, shards):
    rows = own.shape[1]
    one_sided, turns, sent = row_plan(rows, shards)
    place = lax.axis_index("rows")
    if one_sided:
        start = jnp.where(place == 0, rows - sent, 0)
        block = lax.dynamic_slice_in_dim(own, start, sent, axis=1)
        got = lax.ppermute(block, "rows", [(0, 1), (1, 0)])
        first = jnp.where(place == 0, rows, -sent)
        return (got, first + jnp.arange(sent))
    pieces, where = [], []
    for turn in range(turns, 0, -1):
        pieces.append(lax.ppermute(own[:, rows - sent :], "rows", route(shards, turn)))
        where.append(jnp.arange(sent) - (turn - 1) * rows - sent)
    for turn in range(1, turns + 1):
        pieces.append(lax.ppermute(own[:, :sent], "rows", route(shards, -turn)))
        where.append(jnp.arange(sent) + turn * rows)
    return (jnp.concatenate(pieces, axis=1), jnp.concatenate(where))


def return_rows(own, borrowed, shards):
    rows = own.shape[1]
    one_sided, turns, sent = row_plan(rows, shards)
    place = lax.axis_index("rows")
    borrowed = borrowed.astype(jnp.bfloat16)
    if one_sided:
        got = lax.ppermute(borrowed, "rows", [(0, 1), (1, 0)]).astype(own.dtype)
        room = [(0, 0)] * own.ndim
        at_end, at_start = list(room), list(room)
        at_end[1], at_start[1] = (rows - sent, 0), (0, rows - sent)
        return own + jnp.where(place == 0, jnp.pad(got, at_end), jnp.pad(got, at_start))
    piece = 0
    for turn in range(turns, 0, -1):
        back = lax.ppermute(borrowed[:, piece * sent : (piece + 1) * sent], "rows", route(shards, -turn))
        own = own.at[:, rows - sent :].add(back.astype(own.dtype))
        piece += 1
    for turn in range(1, turns + 1):
        back = lax.ppermute(borrowed[:, piece * sent : (piece + 1) * sent], "rows", route(shards, turn))
        own = own.at[:, :sent].add(back.astype(own.dtype))
        piece += 1
    return own


def head_window(head):
    first, last = head * HEAD_DIM, (head + 1) * HEAD_DIM
    return (first // LANES * LANES, -(-last // LANES) * LANES)


def head_mask(head, dtype):
    low, high = head_window(head)
    lane = lax.broadcasted_iota(jnp.int32, (1, high - low), 1) + low
    return ((lane >= head * HEAD_DIM) & (lane < (head + 1) * HEAD_DIM)).astype(dtype)


def nt_dot(left, right):
    return lax.dot_general(left, right, (((1,), (1,)), ((), ())), preferred_element_type=jnp.float32)


def tn_dot(left, right):
    return lax.dot_general(left, right, (((0,), (0,)), ((), ())), preferred_element_type=jnp.float32)


def attend_kernel(mixed_ref, table_ref, out_ref, acc_ref, *, own, total):
    def columns(part, low, high, count):
        block = mixed_ref[0, : count // GRID, 0, :, part * D + low : part * D + high]
        return block.reshape(count, high - low)

    for head in range(HEADS):
        low, high = head_window(head)
        keep = head_mask(head, jnp.bfloat16)
        query = columns(0, low, high, own) * keep
        scores = nt_dot(query, columns(1, low, high, total)) * score_scale + table_ref[head]
        top = jnp.max(scores, axis=1, keepdims=True)
        weight = jnp.exp(scores - top)
        weight = weight * (1.0 / jnp.sum(weight, axis=1, keepdims=True))
        result = low_dot(weight.astype(jnp.bfloat16), columns(2, low, high, total))
        mine = head_mask(head, jnp.float32)
        if head == 0:
            acc_ref[:, low:high] = result
        else:
            earlier = acc_ref[:, low : low + LANES]
            acc_ref[:, low : low + LANES] = jnp.where(mine[:, :LANES] > 0, result[:, :LANES], earlier)
            if high - low > LANES:
                acc_ref[:, low + LANES : high] = result[:, LANES:]
    out_ref[0, :, 0] = acc_ref[...].astype(jnp.bfloat16).reshape(own // GRID, GRID, D)


def attend_back_kernel(mixed_ref, grad_ref, table_ref, out_ref, bias_ref, q_ref, k_ref, v_ref, *, own, total):
    @pl.when((pl.program_id(0) == 0) & (pl.program_id(1) == 0))
    def _():
        bias_ref[...] = jnp.zeros_like(bias_ref)

    def columns(part, low, high, count):
        block = mixed_ref[0, : count // GRID, 0, :, part * D + low : part * D + high]
        return block.reshape(count, high - low)

    def put(ref, low, high, value, fresh):
        if fresh:
            ref[:, low:high] = value
        else:
            ref[:, low : low + LANES] += value[:, :LANES]
            if high - low > LANES:
                ref[:, low + LANES : high] = value[:, LANES:]

    for head in range(HEADS):
        low, high = head_window(head)
        fresh = head * HEAD_DIM % LANES == 0
        keep = head_mask(head, jnp.bfloat16)
        query = columns(0, low, high, own) * keep
        grad = grad_ref[0, :, 0, :, low:high].reshape(own, high - low) * keep
        keys = columns(1, low, high, total)
        scores = nt_dot(keys, query) * score_scale + table_ref[head]
        top = jnp.max(scores, axis=0, keepdims=True)
        weight = jnp.exp(scores - top)
        weight = weight * (1.0 / jnp.sum(weight, axis=0, keepdims=True))
        grad_weight = nt_dot(columns(2, low, high, total), grad)
        delta = jnp.sum(weight * grad_weight, axis=0, keepdims=True)
        grad_scores = weight * (grad_weight - delta)
        bias_ref[head] += grad_scores
        grad_low = grad_scores.astype(jnp.bfloat16)
        put(v_ref, low, high, low_dot(weight.astype(jnp.bfloat16), grad), fresh)
        put(k_ref, low, high, low_dot(grad_low, query), fresh)
        put(q_ref, low, high, tn_dot(grad_low, keys) * head_mask(head, jnp.float32), fresh)
    rows, own_rows = total // GRID, own // GRID
    out_ref[0, :own_rows, 0, :, :D] = (q_ref[...] * score_scale).astype(jnp.bfloat16).reshape(own_rows, GRID, D)
    if rows > own_rows:
        out_ref[0, own_rows:, 0, :, :D] = jnp.zeros((rows - own_rows, GRID, D), jnp.bfloat16)
    out_ref[0, :, 0, :, D : 2 * D] = (k_ref[...] * score_scale).astype(jnp.bfloat16).reshape(rows, GRID, D)
    out_ref[0, :, 0, :, 2 * D :] = v_ref[...].astype(jnp.bfloat16).reshape(rows, GRID, D)


def attend(mixed, table, own_rows):
    seqs, rows = mixed.shape[:2]
    own, total = own_rows * GRID, rows * GRID
    return pl.pallas_call(
        functools.partial(attend_kernel, own=own, total=total),
        grid=(seqs, PACK),
        in_specs=[
            pl.BlockSpec((1, rows, 1, GRID, 3 * D), lambda s, p: (s, 0, p, 0, 0)),
            pl.BlockSpec((HEADS, own, total), lambda s, p: (0, 0, 0)),
        ],
        out_specs=pl.BlockSpec((1, own_rows, 1, GRID, D), lambda s, p: (s, 0, p, 0, 0)),
        out_shape=jax.ShapeDtypeStruct((seqs, own_rows, PACK, GRID, D), jnp.bfloat16),
        scratch_shapes=[pltpu.VMEM((own, D), jnp.float32)],
        compiler_params=pltpu.CompilerParams(
            dimension_semantics=("arbitrary", "arbitrary"), vmem_limit_bytes=48 << 20
        ),
        name="attend",
    )(mixed, table)


def attend_back(mixed, grad, table, own_rows):
    seqs, rows = mixed.shape[:2]
    own, total = own_rows * GRID, rows * GRID
    return pl.pallas_call(
        functools.partial(attend_back_kernel, own=own, total=total),
        grid=(seqs, PACK),
        in_specs=[
            pl.BlockSpec((1, rows, 1, GRID, 3 * D), lambda s, p: (s, 0, p, 0, 0)),
            pl.BlockSpec((1, own_rows, 1, GRID, D), lambda s, p: (s, 0, p, 0, 0)),
            pl.BlockSpec((HEADS, total, own), lambda s, p: (0, 0, 0)),
        ],
        out_specs=[
            pl.BlockSpec((1, rows, 1, GRID, 3 * D), lambda s, p: (s, 0, p, 0, 0)),
            pl.BlockSpec((HEADS, total, own), lambda s, p: (0, 0, 0)),
        ],
        out_shape=[
            jax.ShapeDtypeStruct((seqs, rows, PACK, GRID, 3 * D), jnp.bfloat16),
            jax.ShapeDtypeStruct((HEADS, total, own), jnp.float32),
        ],
        scratch_shapes=[
            pltpu.VMEM((own, D), jnp.float32),
            pltpu.VMEM((total, D), jnp.float32),
            pltpu.VMEM((total, D), jnp.float32),
        ],
        compiler_params=pltpu.CompilerParams(
            dimension_semantics=("arbitrary", "arbitrary"), vmem_limit_bytes=48 << 20
        ),
        name="attend_back",
    )(mixed, grad, table)


def on_device(
    row_shards,
    tokens,
    image_ids,
    timestep,
    norm1_gain,
    norm1_shift,
    time_in_weight,
    time_in_bias,
    time_out_weight,
    time_out_bias,
    mix_weight,
    time_mix_weight,
    position_bias,
    proj_weight,
    proj_bias,
    norm2_gain,
    norm2_shift,
    up_weight,
    up_bias,
    down_weight,
    down_bias,
    cotangent,
):
    seq_rows, local_rows, columns, _ = tokens.shape
    act_tokens = tokens.reshape(seq_rows, local_rows, PACK, GRID, D)
    act_cot = cotangent.reshape(seq_rows, local_rows, PACK, GRID, D)
    token_count = seq_rows * local_rows * columns
    borrowed, borrowed_at = borrow_rows(act_tokens, row_shards)
    ext_tokens = jnp.concatenate([act_tokens, borrowed], axis=1)
    ext_rows = ext_tokens.shape[1]
    ext_count = seq_rows * ext_rows * columns
    full_mix, full_tin, full_tout, full_tmix, full_proj, full_up, full_down = (
        lax.all_gather(mix_weight, "seq", axis=0, tiled=True),
        lax.all_gather(time_in_weight, "seq", axis=0, tiled=True),
        lax.all_gather(time_out_weight, "seq", axis=0, tiled=True),
        lax.all_gather(time_mix_weight, "seq", axis=0, tiled=True),
        lax.all_gather(proj_weight, "seq", axis=0, tiled=True),
        lax.all_gather(up_weight, "seq", axis=0, tiled=True),
        lax.all_gather(down_weight, "seq", axis=0, tiled=True),
    )

    key_at = jnp.concatenate([jnp.arange(local_rows), borrowed_at])
    row_diff = key_at[None, :] - jnp.arange(local_rows)[:, None]
    key_row = lax.axis_index("rows") * local_rows + key_at
    row_valid = (key_row >= 0) & (key_row < GRID)
    col_diff = jnp.arange(GRID)[None, :] - jnp.arange(GRID)[:, None]
    offsets = jnp.arange(2 * REACH + 1) - REACH
    row_hot = (row_diff[:, :, None] == offsets[None, None, :]).astype(jnp.float32)
    col_hot = (col_diff[:, :, None] == offsets[None, None, :]).astype(jnp.float32)
    allowed = (
        (jnp.abs(row_diff) <= REACH)[:, None, :, None]
        & row_valid[None, None, :, None]
        & (jnp.abs(col_diff) <= REACH)[None, :, None, :]
    )
    own, total = local_rows * GRID, ext_rows * GRID
    table = jnp.einsum("hno,abn,ceo->hacbe", position_bias, row_hot, col_hot, precision=highest)
    table = jnp.where(allowed, table, floor_score).reshape(HEADS, own, total)
    table_back = jnp.swapaxes(table, 1, 2)

    half_width = FREQ // 2
    frequency = jnp.exp(-math.log(10000.0) * jnp.arange(half_width, dtype=jnp.float32) / half_width)
    angles = timestep.astype(jnp.float32)[:, :, None] * frequency
    features = jnp.concatenate([jnp.cos(angles), jnp.sin(angles)], axis=-1).astype(jnp.bfloat16)
    time_pre = low_dot(features, full_tin) + time_in_bias
    time_hidden = jax.nn.silu(time_pre).astype(jnp.bfloat16)
    time_embed = (low_dot(time_hidden, full_tout) + time_out_bias).astype(jnp.bfloat16)
    time_proj = low_dot(time_embed, full_tmix)
    block_slots = image_ids[:, ::GRID]
    slot_hot = (block_slots[:, :, None] == jnp.arange(PACK, dtype=jnp.int32)[None, None, :]).astype(
        jnp.float32
    )
    unit_total = seq_rows * PACK
    unit_time = jnp.einsum("skp,spe->ske", slot_hot, time_proj, precision=highest)

    ext_float = ext_tokens.astype(jnp.float32)
    normed1, unit_one, inverse_one = norm_forward(ext_float, norm1_gain, norm1_shift)
    normed1 = normed1.astype(jnp.bfloat16)
    unit_one, inverse_one = unit_one[:, :local_rows], inverse_one[:, :local_rows]
    mixed = (low_dot(normed1, full_mix) + unit_time[:, None, :, None, :]).astype(jnp.bfloat16)
    attended = attend(mixed, table, local_rows)

    flat_tokens = act_tokens.astype(jnp.float32)
    branch = low_dot(attended, full_proj) + proj_bias
    residual = flat_tokens + branch
    normed2, unit_two, inverse_two = norm_forward(residual, norm2_gain, norm2_shift)
    normed2 = normed2.astype(jnp.bfloat16)
    hidden_pre = low_dot(normed2, full_up) + up_bias
    hidden = gelu_tanh(hidden_pre).astype(jnp.bfloat16)
    output = (residual + low_dot(hidden, full_down) + down_bias).astype(jnp.bfloat16)
    flat_hidden = hidden.reshape(token_count, FF)
    flat_cot = act_cot.reshape(token_count, D)
    grad_down_w = jnp.einsum("nf,nd->fd", flat_hidden, flat_cot, preferred_element_type=jnp.float32)
    grad_down_b = jnp.sum(flat_cot, axis=0, dtype=jnp.float32)
    grad_hidden = jnp.einsum("nd,fd->nf", flat_cot, full_down, preferred_element_type=jnp.float32)
    gelu_back = jax.vjp(gelu_tanh, hidden_pre.reshape(token_count, FF))[1]
    grad_pre = gelu_back(grad_hidden)[0].astype(jnp.bfloat16)
    flat_normed2 = normed2.reshape(token_count, D)
    grad_up_w = jnp.einsum("nd,nf->df", flat_normed2, grad_pre, preferred_element_type=jnp.float32)
    grad_up_b = jnp.sum(grad_pre, axis=0, dtype=jnp.float32)
    grad_normed2 = jnp.einsum(
        "nf,df->nd", grad_pre, full_up, preferred_element_type=jnp.float32
    ).reshape(act_tokens.shape)
    grad_norm_two, grad_gain_two, grad_shift_two = norm_backward(
        grad_normed2, unit_two, inverse_two, norm2_gain
    )
    grad_residual = act_cot.astype(jnp.float32) + grad_norm_two
    grad_branch = grad_residual.astype(jnp.bfloat16).reshape(token_count, D)
    grad_proj_w = jnp.einsum(
        "nd,ne->de",
        attended.reshape(token_count, D),
        grad_branch,
        preferred_element_type=jnp.float32,
    )
    grad_proj_b = jnp.sum(grad_branch, axis=0, dtype=jnp.float32)
    grad_attended = jnp.einsum(
        "ne,de->nd", grad_branch, full_proj, preferred_element_type=jnp.float32
    ).astype(jnp.bfloat16)

    grad_mixed, grad_table = attend_back(
        mixed, grad_attended.reshape(act_tokens.shape), table_back, local_rows
    )
    grad_table = grad_table.reshape(HEADS, ext_rows, GRID, local_rows, GRID)
    col_summed = jnp.einsum("hbeac,ceo->hbao", grad_table, col_hot, precision=highest)
    bias_grad = jnp.einsum("hbao,abn->hno", col_summed, row_hot, precision=highest)

    flat_mixed = grad_mixed.reshape(ext_count, 3 * D)
    grad_mix_w = jnp.einsum(
        "nd,ne->de", normed1.reshape(ext_count, D), flat_mixed, preferred_element_type=jnp.float32
    )
    grad_normed1 = jnp.einsum(
        "ne,de->nd", flat_mixed, full_mix, preferred_element_type=jnp.float32
    ).reshape(ext_tokens.shape)
    grad_normed1 = return_rows(
        grad_normed1[:, :local_rows], grad_normed1[:, local_rows:], row_shards
    )
    grad_unit = jnp.sum(grad_mixed, axis=(1, 3), dtype=jnp.float32)
    grad_time_proj = jnp.einsum("skp,ske->spe", slot_hot, grad_unit, precision=highest)
    grad_tmix_w = jnp.einsum(
        "spd,spe->de", time_embed.astype(jnp.float32), grad_time_proj, precision=highest
    )
    grad_embed = jnp.einsum(
        "spe,de->spd", grad_time_proj, full_tmix.astype(jnp.float32), precision=highest
    )
    grad_tout_w = jnp.einsum(
        "spd,spe->de", time_hidden.astype(jnp.float32), grad_embed, precision=highest
    )
    grad_tout_b = jnp.sum(grad_embed, axis=(0, 1))
    grad_thidden = jnp.einsum(
        "spe,de->spd", grad_embed, full_tout.astype(jnp.float32), precision=highest
    )
    silu_back = jax.vjp(jax.nn.silu, time_pre)[1]
    grad_tpre = silu_back(grad_thidden)[0]
    grad_tin_w = jnp.einsum(
        "spf,spd->fd", features.astype(jnp.float32), grad_tpre, precision=highest
    )
    grad_tin_b = jnp.sum(grad_tpre, axis=(0, 1))
    grad_norm_one, grad_gain_one, grad_shift_one = norm_backward(
        grad_normed1, unit_one, inverse_one, norm1_gain
    )
    tokens_grad = (grad_residual + grad_norm_one).astype(jnp.bfloat16)

    def scattered(grad):
        part = lax.psum_scatter(grad.astype(jnp.bfloat16), "seq", scatter_dimension=0, tiled=True)
        return lax.psum(part, "rows").astype(jnp.float32)

    sum_down, sum_up, sum_proj, sum_tin, sum_tout, sum_tmix, sum_mix = (
        scattered(grad_down_w),
        scattered(grad_up_w),
        scattered(grad_proj_w),
        scattered(grad_tin_w),
        scattered(grad_tout_w),
        scattered(grad_tmix_w),
        scattered(grad_mix_w),
    )
    (
        gain_one,
        shift_one,
        tin_bias,
        tout_bias,
        bias_total,
        proj_total,
        gain_two,
        shift_two,
        up_total,
        down_total,
    ) = lax.psum(
        (
            grad_gain_one,
            grad_shift_one,
            grad_tin_b,
            grad_tout_b,
            bias_grad,
            grad_proj_b,
            grad_gain_two,
            grad_shift_two,
            grad_up_b,
            grad_down_b,
        ),
        ("seq", "rows"),
    )
    output = output.reshape(tokens.shape)
    tokens_grad = tokens_grad.reshape(tokens.shape)
    return (
        output,
        tokens_grad,
        gain_one,
        shift_one,
        sum_tin,
        tin_bias,
        sum_tout,
        tout_bias,
        sum_mix,
        sum_tmix,
        bias_total,
        sum_proj,
        proj_total,
        gain_two,
        shift_two,
        sum_up,
        up_total,
        sum_down,
        down_total,
    )


def solution(mesh):
    whole, sharded = (P(), P("seq", None))
    acts = P("seq", "rows", None, None)
    return jax.shard_map(
        functools.partial(on_device, mesh.shape["rows"]),
        mesh=mesh,
        in_specs=(
            acts,
            sharded,
            sharded,
            whole,
            whole,
            sharded,
            whole,
            sharded,
            whole,
            sharded,
            sharded,
            whole,
            sharded,
            whole,
            whole,
            whole,
            sharded,
            whole,
            sharded,
            whole,
            acts,
        ),
        out_specs=(
            acts,
            acts,
            whole,
            whole,
            sharded,
            whole,
            sharded,
            whole,
            sharded,
            sharded,
            whole,
            sharded,
            whole,
            whole,
            whole,
            sharded,
            whole,
            sharded,
            whole,
        ),
        check_vma=False,
    )
```

time: 2000 us -> 1240 us (0.62)
  matrix products: 668 us -> 256 us
  local copies, waits for them, and re-layouts: 249 us -> 41.4 us
  other arithmetic: 235 us -> 57.1 us
  Pallas kernels: 0 us -> 87.5 us
  loops' own time: 26.6 us -> 0 us
    dot_general x20 -> x4, matrix products: 454 us -> 28.9 us  [the longest x1 19.5 us: on_device(): jnp.einsum('nd,ne->de', normed1.reshape(ext_count, D), flat_mixed, prefer...]
    reduce_sum x6 -> x1, other arithmetic: 171 us -> 5.61 us  [on_device(): grad_unit = jnp.sum(grad_mixed, axis=(1, 3), dtype=jnp.float32)]
    pallas_call x0 -> x2, Pallas kernels: none -> 87.5 us  [the longest x1 44.7 us: attend(): pl.pallas_call(functools.partial(attend_kernel, own=own, total=total), gr...]
    reshape x7 -> x3, local copies, waits for them, and re-layouts: 91.9 us -> 16.3 us  [the longest x2 9.73 us: on_device(): table = jnp.where(allowed, table, floor_score).reshape(HEADS, own, total)]
    ppermute x8 -> x2, waiting for transfers between devices: 66.9 us -> 0.01 us  [the longest x1 0.01 us: borrow_rows(): got = lax.ppermute(block, 'rows', [(0, 1), (1, 0)])]
    all_gather x1, waiting for transfers between devices: 0.01 us -> 65.3 us  [on_device(): lax.all_gather(down_weight, 'seq', axis=0, tiled=True)]
    all_gather x1, waiting for transfers between devices: 0.01 us -> 54.1 us  [on_device(): lax.all_gather(up_weight, 'seq', axis=0, tiled=True)]
    psum x1, waiting for transfers between devices: 59.8 us -> 10.7 us  [scattered(): return lax.psum(part, 'rows').astype(jnp.float32)]
  transfers between devices with their start and end apart: 22 -> 16, of which waited for: 12 -> 10; matrix products, arithmetic and copies ran while one was open for 27% -> 22% of each run, Pallas kernels for 0% -> 7%
where the time goes in v1:
time: 1240 us
  waiting for transfers between devices  695 us (56%)
  matrix products  256 us (21%)
  Pallas kernels  87.5 us (7%)
  blocking collectives  79.1 us (6%)
  other arithmetic  57.1 us (5%)
  local copies, waits for them, and re-layouts  41.4 us (3%)
  between operations  15 us (1%)
    reduce_scatter x3, waiting for transfers between devices, scattered(): lax.psum_scatter(grad.astype(jnp.bfloat16), 'seq', scatter_dimension=0, t...  297 us
    unnamed x18, waiting for transfers between devices  151 us
    dot_general x7, matrix products, low_dot(): return jnp.dot(left, right, preferred_element_type=jnp.float32)  78.4 us
    all_gather x1, waiting for transfers between devices, on_device(): lax.all_gather(mix_weight, 'seq', axis=0, tiled=True)  67.9 us
    all_gather x1, waiting for transfers between devices, on_device(): lax.all_gather(down_weight, 'seq', axis=0, tiled=True)  65.3 us
    all_gather x1, waiting for transfers between devices, on_device(): lax.all_gather(up_weight, 'seq', axis=0, tiled=True)  54.1 us
    all_gather x1, waiting for transfers between devices, on_device(): lax.all_gather(time_mix_weight, 'seq', axis=0, tiled=True)  48.7 us
    psum x1, blocking collectives, on_device(): lax.psum((grad_gain_one, grad_shift_one, grad_tin_b, grad_tout_b, bias_gr...  45.3 us
  transfers between devices with their start and end apart: 16, of which 10 were waited for; matrix products, arithmetic and copies ran while one was open for 22% of the time, Pallas kernels for 7%

profile of v1, /device:TPU:0, one launch (start us, length us, event | category | flops | bytes accessed | tf_op | source)
XLA Modules:
  0.0 1236.5 jit_solution(11543637698765964476)
XLA Ops:
  11.2 2.4 constant_dynamic-slice_fusion
  13.6 2.9 collective-permute-start
  17.8 8.6 bitcast_select_fusion
  26.3 13.1 %copy.45 = f32[16,8,16,12,16]{2,1,4,3,0:T(8,128)} copy(f32[16,8,16,12,16]{4,0,2,3,1:T(8,128)} %bitcast_select_fusion) | data formatting | bytes 3145728 | tf_op jit(solution)/shard_map/jit(_where)/select_n | solution.py:304
  39.5 7.9 reshape.253
  47.4 1.8 copy.46.table_ref
  49.4 24.6 %all_gather.22 = bf16[256,1152]{1,0:T(8,128)(2,1)S(1)} all-gather(bf16[16,1152]{1,0:T(8,128)(2,1)S(1)} %copy-done.34), channel_id=1, replica_groups=mesh['seq'=16,'rows'=2] {'seq'}, dimensions={0}, use_global_device_ids=true | all-gather | bytes 626688 | tf_op jit(solution)/shard_map/all_gather | solution.py:281
  74.3 2.7 convert_reduce_fusion.2
  77.0 1.2 fusion.33
  78.9 2.3 fusion.52
  81.2 48.7 %all-gather.11.cloned.1.call-done = bf16[1152,3456]{1,0:T(8,128)(2,1)} async-done(((bf16[72,3456]{1,0:T(8,128)(2,1)}), bf16[1152,3456]{1,0:T(8,128)(2,1)}) %all-gather.11.cloned.1.call-update) | async-done | bytes 7962640 | tf_op jit(solution)/shard_map/all_gather | solution.py:283
  129.9 4.5 fusion.29
  134.7 67.9 %all-gather.7.cloned.1.call-done = bf16[1152,3456]{1,0:T(8,128)(2,1)} async-done(((bf16[72,3456]{1,0:T(8,128)(2,1)}), bf16[1152,3456]{1,0:T(8,128)(2,1)}) %all-gather.7.cloned.1.call-update) | async-done | bytes 7962640 | tf_op jit(solution)/shard_map/all_gather | solution.py:280
  202.7 21.2 %add_convert_fusion.mixed_ref = bf16[2,12,4,16,3456]{4,3,2,1,0:T(8,128)(2,1)} fusion(f32[2,4,3456]{2,1,0:T(4,128)S(1)} %fusion.73, bf16[1152,3456]{1,0:T(8,128)(2,1)} %all-gather.7.cloned.1.call-done, f32[1152]{0:T(1024)S(1)} %copy-done.56, f32[1152]{0:T(1024)S(1)} %copy-done.35, f32[2,12,4,16]{3,2,1,0:T(4,128)S(1)} %get-tuple-element.94, ...), kind=kOutput, calls=%fused_computation.4 | convolution fusion | flops 12253593600 | bytes 22250496 | tf_op jit(solution)/shard_map/dot_general | solution.py:29
  224.0 44.7 %attend.1 = bf16[2,8,4,16,1152]{4,3,2,1,0:T(8,128)(2,1)S(1)} custom-call(bf16[2,12,4,16,3456]{4,3,2,1,0:T(8,128)(2,1)} %add_convert_fusion.mixed_ref, f32[16,128,192]{2,1,0:T(8,128)S(1)} %copy-done), custom_call_target="tpu_custom_call" | custom-call | tf_op jit(solution)/shard_map/attend/pallas_call | solution.py:199
  268.7 1.4 copy-done.1
  270.1 6.9 fusion.84
  277.7 1.4 copy-done.3
  279.7 2.2 add_convert_fusion.3
  282.0 54.1 %all-gather.15.cloned.1.call-done = bf16[1152,4608]{1,0:T(8,128)(2,1)} async-done(((bf16[72,4608]{1,0:T(8,128)(2,1)}), bf16[1152,4608]{1,0:T(8,128)(2,1)}) %all-gather.15.cloned.1.call-update) | async-done | bytes 10616848 | tf_op jit(solution)/shard_map/all_gather | solution.py:285
  336.1 23.7 %fusion.14 = (bf16[2,8,4,16,4608]{4,3,2,1,0:T(8,128)(2,1)}, f32[2,8,4,16,4608]{4,3,2,1,0:T(8,128)}) fusion(f32[4608]{0:T(1024)S(1)} %copy-done.54, bf16[2,8,4,16,1152]{4,3,2,1,0:T(8,128)(2,1)} %add_convert_fusion.3, bf16[1152,4608]{1,0:T(8,128)(2,1)} %all-gather.15.cloned.1.call-done), kind=kOutput, calls=%fused_computation.21 | convolution fusion | flops 10918821888 | bytes 41306112 | tf_op jit(solution)/shard_map/dot_general | solution.py:29
  359.8 65.3 %all-gather.17.cloned.1.call-done = bf16[4608,1152]{1,0:T(8,128)(2,1)} async-done(((bf16[288,1152]{1,0:T(8,128)(2,1)}), bf16[4608,1152]{1,0:T(8,128)(2,1)}) %all-gather.17.cloned.1.call-update) | async-done | bytes 10616848 | tf_op jit(solution)/shard_map/all_gather | solution.py:286
  425.1 29.9 %convert_reduce_fusion.1 = (f32[4608]{0:T(1024)}, bf16[1024,4608]{1,0:T(8,128)(2,1)}) fusion(f32[2,8,4,16,4608]{4,3,2,1,0:T(8,128)} %get-tuple-element.100, bf16[1024,1152]{1,0:T(8,128)(2,1)} %bitcast.182, bf16[4608,1152]{1,0:T(8,128)(2,1)} %all-gather.17.cloned.1.call-done), kind=kOutput, calls=%fused_computation.25 | convolution fusion | flops 10975440896 | bytes 41306112 | tf_op jit(solution)/shard_map/nd,fd->nf/dot_general | solution.py:341
  455.0 20.2 %fusion.82 = (f32[1152]{0:T(1024)}, f32[1024]{0:T(1024)S(1)}, f32[1024,1152]{1,0:T(8,128)}) fusion(f32[1152]{0:T(1024)S(1)} %copy-done.28, bf16[1024,4608]{1,0:T(8,128)(2,1)} %get-tuple-element.86, bf16[1152,4608]{1,0:T(8,128)(2,1)} %all-gather.15.cloned.1.call-done), kind=kOutput, calls=%fused_computation.139 | convolution fusion | flops 10875172864 | bytes 24785920 | tf_op jit(solution)/shard_map/nf,df->nd/dot_general | solution.py:347
  475.2 5.8 multiply_reduce_fusion
  481.1 7.6 convert_reduce_fusion.3
  488.7 1.4 copy-done.10
  490.1 4.8 fusion.32
  495.0 6.1 convolution_convert_fusion.2
  501.1 42.7 %attend_back.1 = (bf16[2,12,4,16,3456]{4,3,2,1,0:T(8,128)(2,1)}, f32[16,192,128]{2,1,0:T(8,128)S(1)}) custom-call(bf16[2,12,4,16,3456]{4,3,2,1,0:T(8,128)(2,1)} %add_convert_fusion.mixed_ref, bf16[2,8,4,16,1152]{4,3,2,1,0:T(8,128)(2,1)S(1)} %bitcast.171, f32[16,192,128]{2,1,0:T(8,128)S(1)} %bitcast.170), custom_call_target="tpu_custom_call" | custom-call | tf_op jit(solution)/shard_map/attend_back/pallas_call | solution.py:219
  543.9 5.6 convert_reduce_fusion
  549.8 6.5 fusion.86
  556.3 3.8 fusion.31
  560.3 19.5 %fusion.17 = bf16[1152,3456]{1,0:T(8,128)(2,1)} fusion(bf16[2,12,4,16,3456]{4,3,2,1,0:T(8,128)(2,1)} %get-tuple-element.21, f32[1152]{0:T(1024)S(1)} %copy-done.57, f32[1152]{0:T(1024)S(1)} %copy-done.36, f32[2,12,4,16]{3,2,1,0:T(4,128)S(1)} %copy-done.23, f32[2,12,4,16]{3,2,1,0:T(4,128)S(1)} %copy-done.19, bf16[2,4,4,16,1152]{4,3,2,1,0:T(8,128)(2,1)S(1)} %copy-done.8, ...), kind=kOutput, calls=%fused_computation.28 | convolution fusion | flops 12246958080 | bytes 22139904 | tf_op jit(solution)/shard_map/nd,ne->de/dot_general | solution.py:374
  580.5 8.5 fusion.18
  589.1 17.3 %convolution_convert_fusion.1 = bf16[1152,4608]{1,0:T(8,128)(2,1)} fusion(bf16[1024,1152]{1,0:T(8,128)(2,1)} %bitcast.186, bf16[1024,4608]{1,0:T(8,128)(2,1)} %get-tuple-element.86), kind=kOutput, calls=%fused_computation.6 | convolution fusion | flops 10876944384 | bytes 22413312 | tf_op jit(solution)/shard_map/nd,nf->df/dot_general | solution.py:345
  606.5 18.2 %convolution_convert_fusion = bf16[4608,1152]{1,0:T(8,128)(2,1)} fusion(bf16[1024,4608]{1,0:T(8,128)(2,1)} %bitcast.189, bf16[1024,1152]{1,0:T(8,128)(2,1)} %bitcast.184), kind=kOutput, calls=%fused_computation.5 | convolution fusion | flops 10876944384 | bytes 22413312 | tf_op jit(solution)/shard_map/nf,nd->fd/dot_general | solution.py:339
  625.5 2.1 convert_reduce_fusion.4
  627.5 4.6 fusion.22
  632.2 20.4 %fusion.24 = f32[2,12,4,16,1152]{4,3,2,1,0:T(8,128)S(1)} fusion(bf16[2,12,4,16,3456]{4,3,2,1,0:T(8,128)(2,1)} %get-tuple-element.21, bf16[1152,3456]{1,0:T(8,128)(2,1)} %all-gather.7.cloned.1.call-done), kind=kOutput, calls=%fused_computation.41 | convolution fusion | flops 12230590464 | bytes 25657344 | tf_op jit(solution)/shard_map/ne,de->nd/dot_general | solution.py:377
  652.6 1.3 slice.31
  653.9 1.6 collective-permute-start.1
  655.6 2.3 fusion.85
  657.9 1.5 fusion.48
  659.7 19.7 %fusion.40 = bf16[2,8,4,16,1152]{4,3,2,1,0:T(8,128)(2,1)} fusion(f32[2,8,4,16,1152]{4,3,2,1,0:T(8,128)} %copy-done.3, bf16[2,8,4,16,4608]{4,3,2,1,0:T(8,128)(2,1)} %get-tuple-element.99, bf16[4608,1152]{1,0:T(8,128)(2,1)} %all-gather.17.cloned.1.call-done, f32[1152]{0:T(1024)S(1)} %copy-done.58), kind=kOutput, calls=%fused_computation.68 | convolution fusion | flops 10875174912 | bytes 27136512 | tf_op jit(solution)/shard_map/dot_general | solution.py:29
  679.4 6.6 reshape.260
  686.0 42.2 %reduce-scatter.24.cloned.1.call-done = bf16[72,3456]{1,0:T(8,128)(2,1)} async-done(((bf16[1152,3456]{1,0:T(8,128)(2,1)}), bf16[72,3456]{1,0:T(8,128)(2,1)}) %reduce-scatter.24.cloned.1.call-update) | async-done | bytes 497680
  728.2 105.2 %reduce-scatter.26.cloned.1.call-done = bf16[72,3456]{1,0:T(8,128)(2,1)} async-done(((bf16[1152,3456]{1,0:T(8,128)(2,1)}), bf16[72,3456]{1,0:T(8,128)(2,1)}) %reduce-scatter.26.cloned.1.call-update) | async-done | bytes 497680
  833.3 124.2 %reduce-scatter.18.cloned.1.call-done = bf16[72,4608]{1,0:T(8,128)(2,1)} async-done(((bf16[1152,4608]{1,0:T(8,128)(2,1)}), bf16[72,4608]{1,0:T(8,128)(2,1)}) %reduce-scatter.18.cloned.1.call-update) | async-done | bytes 663568 | tf_op jit(solution)/shard_map/reduce_scatter | solution.py:410
  957.5 123.9 %reduce-scatter.20.cloned.1.call-done = bf16[288,1152]{1,0:T(8,128)(2,1)} async-done(((bf16[4608,1152]{1,0:T(8,128)(2,1)}), bf16[288,1152]{1,0:T(8,128)(2,1)}) %reduce-scatter.20.cloned.1.call-update) | async-done | bytes 663568 | tf_op jit(solution)/shard_map/reduce_scatter | solution.py:410
  1081.5 8.1 fusion.58
  1089.5 0.9 copy.60
  1090.5 1.1 convolution_bitcast_fusion.6
  1091.6 48.6 %reduce-scatter.16.cloned.1.call-done = bf16[16,1152]{1,0:T(8,128)(2,1)} async-done(((bf16[256,1152]{1,0:T(8,128)(2,1)}), bf16[16,1152]{1,0:T(8,128)(2,1)}) %reduce-scatter.16.cloned.1.call-update) | async-done | bytes 36880 | tf_op jit(solution)/shard_map/reduce_scatter | solution.py:410
  1140.2 9.1 psum.121
  1150.2 6.3 multiply_reduce_fusion.1
  1156.5 45.3 %all-reduce.6 = (f32[1152]{0:T(1024)}, f32[1152]{0:T(1024)}, f32[1152]{0:T(1024)}, f32[1152]{0:T(1024)}, f32[16,9,9]{0,1,2:T(8,128)S(1)}, /*index=5*/f32[1152]{0...) all-reduce(f32[1152]{0:T(1024)S(1)} %get-tuple-element.61, ...), channel_id=1, replica_groups=mesh['seq'=16,'rows'=2] {'seq','rows'}, use_global_device_ids=true, to_apply=%region_9.10 | all-reduce | flops 15120 | bytes 120960 | tf_op jit(solution)/shard_map/psum | solution.py:433
  1201.9 0.8 copy.47
  1202.7 7.2 add_convert_fusion.2
  1209.8 10.7 all-reduce.10.cloned.1.call-done
  1220.6 2.3 convert_element_type.151
  1222.9 2.2 convert_element_type.154
  1225.1 2.0 convert_element_type.144
  1227.2 1.0 convert_element_type.146
  (187 shorter events, 12.6 us)
Async XLA Ops:
  7.2 9.4 copy-start.52
  7.2 9.4 copy-start.53
  7.2 9.5 copy-start.31
  7.2 71.7 %all-gather.9.cloned.1.call-start = ((), (), s32[]{:S(2)}) async-start(), calls=%async_computation.8 | async-start | bytes 2820096 | tf_op jit(solution)/shard_map/all_gather | solution.py:282
  8.0 122.0 %all-gather.11.cloned.1.call-start = ((), (), s32[]{:S(2)}) async-start(), calls=%async_computation.9 | async-start | bytes 8460288 | tf_op jit(solution)/shard_map/all_gather | solution.py:283
  8.7 194.0 %all-gather.7.cloned.1.call-start = ((), (), s32[]{:S(2)}) async-start(), calls=%async_computation.7 | async-start | bytes 8460288 | tf_op jit(solution)/shard_map/all_gather | solution.py:280
  9.4 260.7 %all-gather.13.cloned.1.call-start = ((), (), s32[]{:S(2)}) async-start(), calls=%async_computation.10 | async-start | bytes 2820096 | tf_op jit(solution)/shard_map/all_gather | solution.py:284
  10.0 326.0 %all-gather.15.cloned.1.call-start = ((), (), s32[]{:S(2)}) async-start(), calls=%async_computation.11 | async-start | bytes 11280384 | tf_op jit(solution)/shard_map/all_gather | solution.py:285
  10.6 414.5 %all-gather.17.cloned.1.call-start = ((), (), s32[]{:S(2)}) async-start(), calls=%async_computation.12 | async-start | bytes 11280384 | tf_op jit(solution)/shard_map/all_gather | solution.py:286
  11.2 674.8 %reduce-scatter.28.cloned.1.call-start = ((), (), s32[]{:S(2)}) async-start(), calls=%async_computation.19 | async-start | bytes 2820096
  13.6 60.6 %collective-permute-start = (bf16[2,4,4,16,1152]{4,3,2,1,0:T(8,128)(2,1)}, bf16[2,4,4,16,1152]{4,3,2,1,0:T(8,128)(2,1)S(1)}, u32[]{:S(2)}, u32[]{:S(2)}) collective-permute-start(bf16[2,4,4,16,1152]{4,3,2,1,0:T(8,128)(2,1)} %constant_dynamic-slice_fusion), channel_id=1, source_target_pairs={{0,1},{1,0},{2,3},{3,2},{4,5},{5,4},{6,7},{7,6},{8,9},{9,8},{10,11... | collective-permute-start | bytes 3538952 | tf_op jit(solution)/shard_map/ppermute | solution.py:72
  16.7 117.8 %copy-start.44 = (s32[2,4]{1,0:T(2,128)}, s32[2,4]{1,0:T(2,128)S(1)}, u32[]{:S(2)}) copy-start(s32[2,4]{1,0:T(2,128)S(1)} %slice.16) | copy-start | bytes 100
  16.8 9.5 copy-start.49
  39.5 9.9 copy-start.34
  39.5 34.6 %copy-start.46 = (f32[1152]{0:T(1024)S(1)}, f32[1152]{0:T(1024)}, u32[]{:S(2)}) copy-start(f32[1152]{0:T(1024)} %param.27) | copy-start | bytes 13828
  49.2 27.8 %copy-start.5 = (bf16[2,8,64,1152]{3,2,1,0:T(8,128)(2,1)S(1)}, bf16[2,8,64,1152]{3,2,1,0:T(8,128)(2,1)}, u32[]{:S(2)}) copy-start(bf16[2,8,64,1152]{3,2,1,0:T(8,128)(2,1)} %param.21) | copy-start | bytes 7077892
  49.2 29.7 %copy-start.47 = (f32[1152]{0:T(1024)S(1)}, f32[1152]{0:T(1024)}, u32[]{:S(2)}) copy-start(f32[1152]{0:T(1024)} %param.29) | copy-start | bytes 13828
  49.4 24.9 %copy-start.40 = (bf16[2,4,128]{2,1,0:T(4,128)(2,1)}, bf16[2,4,128]{2,1,0:T(4,128)(2,1)S(1)}, u32[]{:S(2)}) copy-start(bf16[2,4,128]{2,1,0:T(4,128)(2,1)S(1)} %get-tuple-element.95) | copy-start | bytes 6148
  49.4 24.9 %copy-start.42 = (bf16[2,4,128]{2,1,0:T(4,128)(2,1)}, bf16[2,4,128]{2,1,0:T(4,128)(2,1)S(1)}, u32[]{:S(2)}) copy-start(bf16[2,4,128]{2,1,0:T(4,128)(2,1)S(1)} %get-tuple-element.96) | copy-start | bytes 6148
  74.2 6.9 copy-start.13
  74.3 128.4 %copy-start.7 = (bf16[2,4,4,16,1152]{4,3,2,1,0:T(8,128)(2,1)}, bf16[2,4,4,16,1152]{4,3,2,1,0:T(8,128)(2,1)S(1)}, u32[]{:S(2)}) copy-start(bf16[2,4,4,16,1152]{4,3,2,1,0:T(8,128)(2,1)S(1)} %collective-permute-done) | copy-start | bytes 3538948
  77.0 125.7 %copy-start.18 = (f32[2,12,4,16]{3,2,1,0:T(4,128)}, f32[2,12,4,16]{3,2,1,0:T(4,128)S(1)}, u32[]{:S(2)}) copy-start(f32[2,12,4,16]{3,2,1,0:T(4,128)S(1)} %broadcast_multiply_fusion) | copy-start | bytes 18436
  78.9 123.8 %copy-start.22 = (f32[2,12,4,16]{3,2,1,0:T(4,128)}, f32[2,12,4,16]{3,2,1,0:T(4,128)S(1)}, u32[]{:S(2)}) copy-start(f32[2,12,4,16]{3,2,1,0:T(4,128)S(1)} %get-tuple-element.94) | copy-start | bytes 18436
  81.2 53.2 %copy-start.20 = (bf16[2,4,1152]{2,1,0:T(4,128)(2,1)}, bf16[2,4,1152]{2,1,0:T(4,128)(2,1)S(1)}, u32[]{:S(2)}) copy-start(bf16[2,4,1152]{2,1,0:T(4,128)(2,1)S(1)} %fusion.52) | copy-start | bytes 55300
  81.2 121.5 %copy-start.35 = (f32[1152]{0:T(1024)S(1)}, f32[1152]{0:T(1024)}, u32[]{:S(2)}) copy-start(f32[1152]{0:T(1024)} %param.24) | copy-start | bytes 13828
  81.2 121.5 %copy-start.56 = (f32[1152]{0:T(1024)S(1)}, f32[1152]{0:T(1024)}, u32[]{:S(2)}) copy-start(f32[1152]{0:T(1024)} %param.25) | copy-start | bytes 13828
  202.7 21.3 %copy-start = (f32[16,128,192]{2,1,0:T(8,128)S(1)}, f32[16,128,192]{2,1,0:T(8,128)}, u32[]{:S(2)}) copy-start(f32[16,128,192]{2,1,0:T(8,128)} %copy.46.table_ref) | copy-start | bytes 4718596
  224.0 46.2 %copy-start.55 = (f32[1152]{0:T(1024)S(1)}, f32[1152]{0:T(1024)}, u32[]{:S(2)}) copy-start(f32[1152]{0:T(1024)} %param.34) | copy-start | bytes 13828
  277.7 58.4 %copy-start.54 = (f32[4608]{0:T(1024)S(1)}, f32[4608]{0:T(1024)}, u32[]{:S(2)}) copy-start(f32[4608]{0:T(1024)} %param.38) | copy-start | bytes 55300
  425.1 29.9 %copy-start.28 = (f32[1152]{0:T(1024)S(1)}, f32[1152]{0:T(1024)}, u32[]{:S(2)}) copy-start(f32[1152]{0:T(1024)} %param.35) | copy-start | bytes 13828
  455.0 20.2 %copy-start.4 = (f32[2,8,4,16,1152]{4,3,2,1,0:T(8,128)S(1)}, f32[2,8,4,16,1152]{4,3,2,1,0:T(8,128)}, u32[]{:S(2)}) copy-start(f32[2,8,4,16,1152]{4,3,2,1,0:T(8,128)} %copy-done.3) | copy-start | bytes 14155780
  455.0 20.2 %copy-start.12 = (f32[2,8,4,16]{3,2,1,0:T(4,128)S(1)}, f32[2,8,4,16]{3,2,1,0:T(4,128)}, u32[]{:S(2)}) copy-start(f32[2,8,4,16]{3,2,1,0:T(4,128)} %copy-done.11) | copy-start | bytes 12292
  455.0 20.3 %copy-start.16 = (f32[2,8,4,16]{3,2,1,0:T(4,128)S(1)}, f32[2,8,4,16]{3,2,1,0:T(4,128)}, u32[]{:S(2)}) copy-start(f32[2,8,4,16]{3,2,1,0:T(4,128)} %copy-done.15) | copy-start | bytes 12292
  481.1 9.0 copy-start.2
  494.9 191.0 %reduce-scatter.22.cloned.1.call-start = ((), (), s32[]{:S(2)}) async-start(), calls=%async_computation.16 | async-start | bytes 2820096
  495.0 54.8 %slice-start = ((s8[7962624]{0:T(1024)(128)(4,1)}), s8[4194304]{0:T(1024)(128)(4,1)S(1)}, s32[]{:S(2)}) async-start(s8[7962624]{0:T(1024)(128)(4,1)} %bitcast.172), calls=%async_computation.21 | async-start | bytes 8388608
  501.1 48.6 %slice-start.1 = ((s8[7962624]{0:T(1024)(128)(4,1)}), s8[3768320]{0:T(1024)(128)(4,1)S(1)}, s32[]{:S(2)}) async-start(s8[7962624]{0:T(1024)(128)(4,1)} %bitcast.172), calls=%async_computation.22 | async-start | bytes 7536640
  543.9 5.6 copy-start.45
  549.8 6.6 copy-start.14
  556.3 4.0 copy-start.8
  556.3 3.9 copy-start.19
  556.3 3.9 copy-start.23
  556.3 3.9 copy-start.36
  556.3 3.9 copy-start.57
  560.2 168.0 %reduce-scatter.24.cloned.1.call-start = ((), (), s32[]{:S(2)}) async-start(), calls=%async_computation.17 | async-start | bytes 8460288
  579.8 253.6 %reduce-scatter.26.cloned.1.call-start = ((), (), s32[]{:S(2)}) async-start(), calls=%async_computation.18 | async-start | bytes 8460288
  589.0 368.5 %reduce-scatter.18.cloned.1.call-start = ((), (), s32[]{:S(2)}) async-start(), calls=%async_computation.14 | async-start | bytes 11280384 | tf_op jit(solution)/shard_map/reduce_scatter | solution.py:410
  606.4 475.0 %reduce-scatter.20.cloned.1.call-start = ((), (), s32[]{:S(2)}) async-start(), calls=%async_computation.15 | async-start | bytes 11280384 | tf_op jit(solution)/shard_map/reduce_scatter | solution.py:410
  624.7 515.5 %reduce-scatter.16.cloned.1.call-start = ((), (), s32[]{:S(2)}) async-start(), calls=%async_computation.13 | async-start | bytes 626688 | tf_op jit(solution)/shard_map/reduce_scatter | solution.py:410
  632.2 23.4 %copy-start.6 = (bf16[1152,1152]{1,0:T(8,128)(2,1)S(1)}, bf16[1152,1152]{1,0:T(8,128)(2,1)}, u32[]{:S(2)}) copy-start(bf16[1152,1152]{1,0:T(8,128)(2,1)} %all-gather.9.cloned.1.call-done) | copy-start | bytes 7962628
  652.6 5.3 copy-start.9
  652.6 5.3 copy-start.41
  652.6 5.2 copy-start.43
  652.6 7.0 copy-start.58
  653.9 496.0 %collective-permute-start.1 = (bf16[2,4,4,16,1152]{4,3,2,1,0:T(8,128)(2,1)}, bf16[2,4,4,16,1152]{4,3,2,1,0:T(8,128)(2,1)S(1)}, u32[]{:S(2)}, u32[]{:S(2)}) collective-permute-start(bf16[2,4,4,16,1152]{4,3,2,1,0:T(8,128)(2,1)} %slice.31), channel_id=1, source_target_pairs={{0,1},{1,0},{2,3},{3,2},{4,5},{5,4},{6,7},{7,6},{8,9},{9,8},{10,11... | collective-permute-start | bytes 3538952 | tf_op jit(solution)/shard_map/ppermute | solution.py:91
  659.4 561.1 %all-reduce.10.cloned.1.call-start = ((), (), s32[]{:S(2)}) async-start(), calls=%async_computation.20 | async-start | bytes 5308416 | tf_op jit(solution)/shard_map/psum | solution.py:411
  1081.4 9.0 copy-start.33
  1150.1 6.4 copy-start.37
  1150.2 6.4 copy-start.38
  1150.2 6.4 copy-start.39
  1150.2 6.4 copy-start.51
  1220.6 6.6 copy-start.17
  1220.6 7.6 copy-start.25
  1220.6 8.4 copy-start.24
  (13 other events, 19.5 us)
Sparse Core Ops, SparseCore 0:
  10.2 46.0 all-gather.8
  58.5 71.3 all-gather.10
  132.1 70.5 all-gather.6
  204.7 41.6 all-gather.12
  248.5 87.4 all-gather.14
  338.2 86.8 all-gather.16
  495.0 62.1 reduce-scatter.27
  561.6 62.7 reduce-scatter.21
  628.5 99.6 reduce-scatter.23
  732.6 100.6 reduce-scatter.25
  837.4 120.0 reduce-scatter.17
  961.4 119.9 reduce-scatter.19
  1085.5 54.5 reduce-scatter.15
  1142.8 77.6 all-reduce.9
